TPU v7x, 128 devices: a whole 4x4x4 slice. The times are simulated.
128 devices in a mesh: row: 8 (over z, core), col: 16 (over x, y).
Axes of the slice: x: 4, y: 4, z: 4, core: 2. Of those that a mesh axis runs over, the one named last changes fastest.
Arguments:
- nodes: bfloat16 [65536, 512], P(('row', 'col')), may hold values from -6 to 6
- cotangent: bfloat16 [65536, 512], P(('row', 'col')), may hold values from -6 to 6
- edge_source: int32 [262144], P(('row', 'col')), may hold values from 0 to 639
- edge_target: int32 [262144], P(('row', 'col')), may hold values from 0 to 511
- halo_lists: int32 [128, 4, 32], P(('row', 'col')), may hold values from 0 to 511
- pool_owner: int32 [65536], P(('row', 'col')), may hold values from 0 to 127, as said below
- pool_table: int32 [128, 1024], P(('row', 'col')), may hold values from -1 to 127, as said below
- source_weight: bfloat16 [512, 512], replicated, may hold values from -0.25 to 0.25
- target_weight: bfloat16 [512, 512], replicated, may hold values from -0.25 to 0.25
- edge_weight: bfloat16 [512, 512], replicated, may hold values from -0.25 to 0.25
- inner_weight: bfloat16 [1024, 512], replicated, may hold values from -0.1875 to 0.1875
- outer_weight: bfloat16 [512, 512], replicated, may hold values from -0.25 to 0.25
- coarse_weight: bfloat16 [512, 512], replicated, may hold values from -0.5 to 0.5
Outputs:
- updated: bfloat16 [65536, 512], P(('row', 'col'))
- node_gradient: float32 [65536, 512], P(('row', 'col'))
- source_gradient: float32 [512, 512], replicated
- target_gradient: float32 [512, 512], replicated
- edge_gradient: float32 [512, 512], replicated
- inner_gradient: float32 [1024, 512], replicated
- outer_gradient: float32 [512, 512], replicated
- coarse_gradient: float32 [512, 512], replicated
Inputs may be any that keep to these rules, and one draw needn't show every extreme that they name: `edge_source`: rows below 512 are the partition's own nodes; row 512 + k * 32 + j is row j of halo block k. `pool_owner`: at most 8 nodes of one partition name the same owner; one owner is named by exactly 8 nodes of every partition. `pool_table`: entry [o, q * 8 + k] is the coarse row of owner o for the node of rank k among the nodes of partition q that name o, and -1 where q names o fewer than k + 1 times.
All inputs are finite; a program needn't handle non-finite values.
Results may differ from a plain program's by a relative error of at most 0.014.
Values may be sent and summed in bfloat16 or wider, within the bound.
No kernel may reach another device: no remote copies, remote signals or barrier semaphores. Data moves between devices by JAX's collectives and lax.ppermute only.
A program may use at most 128 MiB of HBM per device.

v0:
```python
import functools
import math

import jax
import jax.numpy as jnp
from jax import lax
from jax.experimental import pallas as pl
from jax.experimental.pallas import tpu as pltpu
from jax.sharding import Mesh
from jax.sharding import PartitionSpec as P


BF = jnp.bfloat16
F32 = jnp.float32
LANES = 128
CHUNK = 1024
CAPACITY = 8
ROW = ("z", "core")
COL = ("x", "y")
CHIPS = ("z", "x", "y")
ALL = ROW + COL


def dot(first, second):
    return jnp.dot(first, second, preferred_element_type=F32)


def left_dot(first, second):
    return lax.dot_general(
        first, second, (((0,), (0,)), ((), ())), preferred_element_type=F32
    )


def right_dot(first, second):
    return lax.dot_general(
        first, second, (((1,), (1,)), ((), ())), preferred_element_type=F32
    )


def iota(shape, axis):
    return lax.broadcasted_iota(jnp.int32, shape, axis)


def column(row):
    square = (row.shape[1],) * 2
    eye = iota(square, 0) == iota(square, 1)
    spread = jnp.broadcast_to(row.astype(F32), square)
    return jnp.sum(jnp.where(eye, spread, 0.0), axis=1, keepdims=True).astype(jnp.int32)


def hot(mask):
    return jnp.where(mask, 1.0, 0.0).astype(BF)


def wide_column(row):
    return jnp.concatenate(
        [column(row[:, k : k + LANES]) for k in range(0, row.shape[1], LANES)], axis=0
    )


def wide_row(ref):
    return jnp.concatenate([ref[k : k + 1, :] for k in range(ref.shape[0])], axis=1)


def gates(value):
    sigma = 0.5 * jnp.tanh(0.5 * value) + 0.5
    active = value * sigma
    return active, sigma + active * (1.0 - sigma)


def sent_order(where):
    return where[0], 1 - where[0], 2 + where[1], 3 - where[1]


def received_order(where):
    return 1 - where[0], where[0], 3 - where[1], 2 + where[1]


def block(at, base, rows):
    return pl.ds(pl.multiple_of(base + at * rows, rows), rows)


def halo_picks(where, lists, rows):
    length = lists.shape[2]
    columns = [column(lists[0, pl.ds(at, 1), :]) for at in sent_order(where)]
    return jnp.concatenate([hot(each == iota((length, rows), 1)) for each in columns], axis=0)


def halo_kernel(where, nodes, lists, *outs):
    picked = dot(halo_picks(where, lists, nodes.shape[0]), nodes[...]).astype(BF)
    rows = outs[0].shape[0]
    for number, out in enumerate(outs):
        out[...] = picked[number * rows : (number + 1) * rows, :]


def prepare_kernel(owner, nodes, source_weight, target_weight, slot_out, own_source, target_side):
    rows = nodes.shape[0]
    owner_row = wide_row(owner)
    owner_column = wide_column(owner_row)
    square = (rows, rows)
    before = (owner_column == owner_row) & (iota(square, 0) < iota(square, 1))
    rank = jnp.sum(jnp.where(before, 1.0, 0.0), axis=0, keepdims=True).astype(jnp.int32)
    slot_out[...] = owner_row * CAPACITY + rank
    own_source[...] = dot(nodes[...], source_weight[...]).astype(BF)
    target_side[...] = dot(nodes[...], target_weight[...]).astype(BF)


def chunk(turn):
    return slice(turn * CHUNK, (turn + 1) * CHUNK)


def forward_kernel(
    where, halo_0, halo_1, halo_2, halo_3, own_source, target_side, nodes, cotangent, edge_source, edge_target, slot,
    source_weight, edge_weight, inner_far, outer_far,
    edge_hidden, edge_slope, message_slope, aggregate, node_hidden, node_slope, refined, sent,
    sides, active, spread, inner_weight, outer_weight, hidden_kept, slope_kept, message_kept, weight_sems, sems,
):
    fetches = [
        pltpu.make_async_copy(inner_far, inner_weight, weight_sems.at[0]),
        pltpu.make_async_copy(outer_far, outer_weight, weight_sems.at[1]),
    ]
    for fetch in fetches:
        fetch.start()
    rows, width = nodes.shape
    extended = rows + LANES
    edges = hidden_kept.shape[0]
    sides[:rows, :] = own_source[...]
    halo = jnp.concatenate([halo_0[...], halo_1[...], halo_2[...], halo_3[...]], axis=0)
    halo = dot(halo, source_weight[...]).astype(BF)
    length = halo_0.shape[0]
    for number, at in enumerate(received_order(where)):
        sides[block(at, rows, length), :] = halo[number * length : (number + 1) * length, :]
    sides[extended:, :] = target_side[...]
    group = CHUNK // LANES
    stores = []
    for turn in range(edges // CHUNK):
        span = chunk(turn)
        picks = []
        for at in range(turn * group, (turn + 1) * group):
            senders = edge_source[at : at + 1, :]
            receivers = edge_target[at : at + 1, :]
            sender_hot = hot(column(senders) == iota((LANES, extended), 1))
            receiver_hot = hot(column(receivers) == iota((LANES, rows), 1))
            picks.append(jnp.concatenate([sender_hot, receiver_hot], axis=1))
            spread[:, at * LANES : (at + 1) * LANES] = hot(iota((rows, LANES), 0) == receivers)
        hidden, slope = gates(dot(jnp.concatenate(picks, axis=0), sides[...]))
        hidden = hidden.astype(BF)
        hidden_kept[span, :] = hidden
        slope_kept[span, :] = slope.astype(BF)
        message, slope = gates(dot(hidden, edge_weight[...]))
        active[span, :] = message.astype(BF)
        message_kept[span, :] = slope.astype(BF)
        pairs = ((hidden_kept, edge_hidden), (slope_kept, edge_slope), (message_kept, message_slope))
        for number, (kept, out) in enumerate(pairs):
            stores.append(pltpu.make_async_copy(kept.at[span, :], out.at[span, :], sems.at[number, turn]))
            stores[-1].start()
    gathered = dot(spread[...], active[...]).astype(BF)
    aggregate[...] = gathered
    for fetch in fetches:
        fetch.wait()
    linear = dot(nodes[...], inner_weight[:width, :]) + dot(gathered, inner_weight[width:, :])
    hidden, slope = gates(linear)
    hidden = hidden.astype(BF)
    node_hidden[...] = hidden
    node_slope[...] = slope.astype(BF)
    result = (nodes[...].astype(F32) + dot(hidden, outer_weight[...])).astype(BF)
    refined[...] = result
    place = hot(iota((sent.shape[0], rows), 0) == slot[...])
    sent[:, :width] = dot(place, result).astype(BF)
    sent[:, width:] = dot(place, cotangent[...]).astype(BF)
    for store in stores:
        store.wait()


def members_kernel(table, members, picks, counts):
    coarse = members.shape[0]
    row = wide_row(table)
    inside = iota((coarse, row.shape[1]), 0) == row
    ones = jnp.where(inside, 1.0, 0.0)
    members[...] = ones.astype(BF)
    count = jnp.maximum(jnp.sum(ones, axis=1, keepdims=True), 1.0)
    counts[...] = jnp.broadcast_to(count, counts.shape)
    picks[...] = hot(wide_column(row) == iota((row.shape[1], coarse), 1))


def coarse_kernel(arrived, members, picks, counts, weight, out, coarse_out, grad_out):
    width = weight.shape[0]
    count = counts[:, :1]
    totals = dot(members[...], arrived[...])
    coarse = (totals[:, :width] / count).astype(BF)
    coarse_out[...] = coarse
    active, slope = gates(dot(coarse, weight[...]))
    grad = (totals[:, width:] * slope).astype(BF)
    grad_out[...] = grad
    share = (right_dot(grad, weight[...]) / count).astype(BF)
    out[:, :width] = dot(picks[...], share).astype(BF)
    out[:, width:] = dot(picks[...], active.astype(BF)).astype(BF)


def half_of(ref, half):
    columns = ref.shape[1] // 2
    return ref[:, pl.ds(pl.multiple_of(half * columns, columns), columns)]


def pack(out, at, value):
    rows, width = value.shape
    for k in range(width // LANES):
        out[at * width // LANES + k * rows : at * width // LANES + (k + 1) * rows, :] = value[
            :, k * LANES : (k + 1) * LANES
        ].astype(BF)


def halves(scale, where, keep, give, pairs):
    at = 0
    for first, second in pairs:
        for out, half in ((keep, where[0]), (give, 1 - where[0])):
            pack(out, at, left_dot(half_of(first, half), second) * scale)
        at += first.shape[1] // 2


def node_back_kernel(
    scale, where, returned, slot, cotangent, nodes, aggregate, node_hidden, node_slope, coarse, grad_coarse,
    inner_weight, outer_weight,
    grad_aggregate, grad_hidden, keep, give,
):
    rows, width = nodes.shape
    picks = hot(wide_column(slot[...]) == iota((rows, returned.shape[0]), 1))
    grad = cotangent[...].astype(F32) + dot(picks, returned[:, :width])
    low = grad.astype(BF)
    hidden = (right_dot(low, outer_weight[...]) * node_slope[...].astype(F32)).astype(BF)
    grad_hidden[...] = hidden
    grad_aggregate[...] = right_dot(hidden, inner_weight[width:, :]).astype(BF)
    pairs = ((node_hidden, low), (nodes, hidden), (aggregate, hidden), (coarse, grad_coarse[...]))
    halves(scale, where, keep, give, pairs)


def edge_back_kernel(
    scale, where, edge_source, edge_target, grad_aggregate, halo_0, halo_1, halo_2, halo_3, nodes, edge_weight,
    source_weight, edge_slope, message_slope, edge_hidden,
    keep, give, grad_sources, grad_targets, back_0, back_1, back_2, back_3,
    slope_kept, message_kept, hidden_kept, grad_message, grad_edges, source_spread, target_spread, extended, sems,
):
    rows, _ = nodes.shape
    table = grad_sources.shape[0]
    edges = slope_kept.shape[0]
    turns = edges // CHUNK
    group = CHUNK // LANES
    fetches = []
    for turn in range(turns):
        span = chunk(turn)
        for number, (far, kept) in enumerate(((message_slope, message_kept), (edge_slope, slope_kept))):
            fetches.append(pltpu.make_async_copy(far.at[span, :], kept.at[span, :], sems.at[number, turn]))
    fetches.append(pltpu.make_async_copy(edge_hidden, hidden_kept, sems.at[2, 0]))
    for fetch in fetches:
        fetch.start()
    extended[:rows, :] = nodes[...]
    length = halo_0.shape[0]
    received = received_order(where)
    for at, halo in zip(received, (halo_0, halo_1, halo_2, halo_3)):
        extended[block(at, rows, length), :] = halo[...]
    for turn in range(turns):
        span = chunk(turn)
        picks = []
        for at in range(turn * group, (turn + 1) * group):
            senders = edge_source[at : at + 1, :]
            receivers = edge_target[at : at + 1, :]
            lanes = slice(at * LANES, (at + 1) * LANES)
            picks.append(hot(column(receivers) == iota((LANES, rows), 1)))
            source_spread[:, lanes] = hot(iota((table, LANES), 0) == senders)
            target_spread[:, lanes] = hot(iota((rows, LANES), 0) == receivers)
        taken = dot(jnp.concatenate(picks, axis=0), grad_aggregate[...])
        fetches[2 * turn].wait()
        message = (taken * message_kept[span, :].astype(F32)).astype(BF)
        grad_message[span, :] = message
        fetches[2 * turn + 1].wait()
        grad = right_dot(message, edge_weight[...]) * slope_kept[span, :].astype(F32)
        grad_edges[span, :] = grad.astype(BF)
    sources = dot(source_spread[...], grad_edges[...]).astype(BF)
    targets = dot(target_spread[...], grad_edges[...]).astype(BF)
    grad_sources[...] = sources
    grad_targets[...] = targets
    back = jnp.concatenate([grad_sources[block(at, rows, length), :] for at in received], axis=0)
    back = right_dot(back, source_weight[...]).astype(BF)
    for number, out in enumerate((back_0, back_1, back_2, back_3)):
        out[...] = back[number * length : (number + 1) * length, :]
    fetches[-1].wait()
    pairs = ((hidden_kept, grad_message[...]), (extended, sources), (nodes, targets))
    halves(scale, where, keep, give, pairs)


def finish_kernel(
    where, returned, slot, cotangent, refined, grad_hidden, grad_sources, grad_targets, lists,
    back_0, back_1, back_2, back_3, inner_weight, source_weight, target_weight,
    updated, node_gradient,
):
    rows, width = refined.shape
    picks = hot(wide_column(slot[...]) == iota((rows, returned.shape[0]), 1))
    updated[...] = (refined[...].astype(F32) + dot(picks, returned[:, width:])).astype(BF)
    back = jnp.concatenate([back_0[...], back_1[...], back_2[...], back_3[...]], axis=0)
    places = halo_picks(where, lists, rows)
    node_gradient[...] = (
        cotangent[...].astype(F32)
        + dot(picks, returned[:, :width])
        + right_dot(grad_hidden[...], inner_weight[:width, :])
        + right_dot(grad_targets[...], target_weight[...])
        + right_dot(grad_sources[:rows, :], source_weight[...])
        + left_dot(places, back)
    )


def results_kernel(early, other, where, gathered, *refs):
    outs, wide, sems = refs[-8:-2], refs[-2], refs[-1]
    source, target, edge, inner, outer, coarse = outs
    which = 1 - where[0] if other else where[0]
    width = wide.shape[1]
    half = width // 2
    blocks = width // LANES
    peers, rows, lanes = gathered.shape
    first = gathered[:, :early, :].astype(F32).reshape(peers * early, lanes)
    second = gathered[:, early:, :].astype(F32).reshape(peers * (rows - early), lanes)
    places = ((outer, 0, first, 0), (inner, 0, first, 1), (inner, width, first, 2), (coarse, 0, first, 3))
    places += ((edge, 0, second, 0), (source, 0, second, 1), (target, 0, second, 2))
    stores = []
    for number, (out, base, values, at) in enumerate(places):
        own = slice(number * half, (number + 1) * half)
        for k in range(blocks):
            start = (at * blocks + k) * half
            wide[own, k * LANES : (k + 1) * LANES] = values[start : start + half, :]
        span = pl.ds(pl.multiple_of(base + which * half, half), half)
        stores.append(pltpu.make_async_copy(wide.at[own, :], out.at[span, :], sems.at[number]))
        stores[-1].start()
    for store in stores:
        store.wait()


def call(kernel, outs, *args, far_in=0, far_out=0, scratch=(), sems=(), where=None, aliases=0, **static):
    body = functools.partial(kernel, *static.values())
    near, far = pl.BlockSpec(memory_space=pltpu.VMEM), pl.BlockSpec(memory_space=pl.ANY)
    specs = [near] * (len(args) - far_in) + [far] * far_in
    if where is not None:
        args, specs = (where,) + args, [pl.BlockSpec(memory_space=pltpu.SMEM)] + specs
    return pl.pallas_call(
        body,
        in_specs=specs,
        out_specs=[far] * far_out + [near] * (len(outs) - far_out),
        out_shape=[jax.ShapeDtypeStruct(shape, dtype) for shape, dtype in outs],
        scratch_shapes=[pltpu.VMEM(shape, dtype) for shape, dtype in scratch]
        + [pltpu.SemaphoreType.DMA(shape) for shape in sems],
        compiler_params=pltpu.CompilerParams(vmem_limit_bytes=32 * 2 ** 20),
        input_output_aliases={len(args) - aliases + k: k for k in range(aliases)},
    )(*args)


def swapped(value, axis, first):
    count = math.prod(lax.axis_size(name) for name in axis)
    lower = range(first, count - 1, 2)
    pairs = [(at, at + 1) for at in lower] + [(at + 1, at) for at in lower]
    return lax.ppermute(value, axis, pairs)


def trade_halo(blocks):
    moved = []
    for number, (axis, first) in enumerate(((ROW, 0), (ROW, 1), (COL, 0), (COL, 1))):
        moved.append(swapped(blocks[number], axis, first))
    return moved


def trade_slots(buffer, devices):
    slots, width = buffer.shape
    shaped = buffer.reshape(devices, slots // devices, width)
    moved = lax.all_to_all(shaped, ALL, split_axis=0, concat_axis=0, tiled=True)
    return moved.reshape(slots, width)


def across(value):
    return lax.ppermute(value, "core", [(0, 1), (1, 0)])


def paired(keep, give):
    return (keep.astype(F32) + across(give).astype(F32)).astype(BF)


def trade_chips(value):
    return lax.all_to_all(value, CHIPS, split_axis=0, concat_axis=0, tiled=True)


def total(arrived):
    return jnp.sum(arrived.astype(F32), axis=0).astype(BF)


def local(
    nodes,
    cotangent,
    edge_source,
    edge_target,
    halo_lists,
    pool_owner,
    pool_table,
    source_weight,
    target_weight,
    edge_weight,
    inner_weight,
    outer_weight,
    coarse_weight,
):
    chips = math.prod(lax.axis_size(name) for name in CHIPS)
    devices = 2 * chips
    where = jnp.stack([lax.axis_index("core"), lax.axis_index("y") % 2])
    rows, width = nodes.shape
    edges = edge_source.shape[0]
    halo_rows = halo_lists.shape[2]
    extended = rows + 4 * halo_rows
    slots = pool_table.shape[1]
    coarse_rows = rows // 4
    scale = 1.0 / math.sqrt(rows * devices)
    owner = pool_owner.reshape(rows // LANES, LANES)
    table = pool_table.reshape(slots // LANES, LANES)
    senders = edge_source.reshape(edges // LANES, LANES)
    receivers = edge_target.reshape(edges // LANES, LANES)
    node_block, edge_block = (rows, width), (edges, width)
    square = ((width, width), F32)
    packed = width // 2 * width // LANES

    halo_blocks = [((halo_rows, width), BF)] * 4
    halo = trade_halo(call(halo_kernel, halo_blocks, nodes, halo_lists, where=where))
    slot, own_source, target_side = call(
        prepare_kernel,
        [((1, rows), jnp.int32), (node_block, BF), (node_block, BF)],
        owner, nodes, source_weight, target_weight,
    )
    edge_hidden, edge_slope, message_slope, aggregate, node_hidden, node_slope, refined, sent = call(
        forward_kernel,
        [(edge_block, BF)] * 3 + [(node_block, BF)] * 4 + [((slots, 2 * width), BF)],
        *halo, own_source, target_side, nodes, cotangent, senders, receivers, slot,
        source_weight, edge_weight, inner_weight, outer_weight,
        far_in=2, far_out=3,
        scratch=[((extended + rows, width), BF), (edge_block, BF), ((rows, edges), BF)]
        + [((2 * width, width), BF), ((width, width), BF)] + [(edge_block, BF)] * 3,
        sems=[(2,), (3, edges // CHUNK)],
        where=where,
    )
    arrived = trade_slots(sent, devices)
    members, picks, counts = call(
        members_kernel,
        [((coarse_rows, slots), BF), ((slots, coarse_rows), BF), ((coarse_rows, LANES), F32)],
        table,
    )
    sent, coarse, grad_coarse = call(
        coarse_kernel,
        [((slots, 2 * width), BF)] + [((coarse_rows, width), BF)] * 2,
        arrived, members, picks, counts, coarse_weight,
    )
    returned = trade_slots(sent, devices)
    grad_aggregate, grad_hidden, keep, give = call(
        node_back_kernel,
        [(node_block, BF), (node_block, BF), ((4 * packed, LANES), BF), ((4 * packed, LANES), BF)],
        returned, slot, cotangent, nodes, aggregate, node_hidden, node_slope, coarse, grad_coarse,
        inner_weight, outer_weight,
        where=where, scale=scale,
    )
    early = paired(keep, give)
    early_rows = 4 * packed // chips
    early = total(trade_chips(early.reshape(chips, early_rows, LANES)))
    keep, give, grad_sources, grad_targets, *back = call(
        edge_back_kernel,
        [((3 * packed, LANES), BF)] * 2 + [((extended, width), BF), (node_block, BF)] + halo_blocks,
        senders, receivers, grad_aggregate, *halo, nodes, edge_weight, source_weight,
        edge_slope, message_slope, edge_hidden,
        far_in=3,
        scratch=[(edge_block, BF)] * 5 + [((extended, edges), BF), ((rows, edges), BF), ((extended, width), BF)],
        sems=[(3, edges // CHUNK)],
        where=where, scale=scale,
    )
    halo_back = trade_halo(back)
    late = paired(keep, give)
    late_rows = 3 * packed // chips
    late = total(trade_chips(late.reshape(chips, late_rows, LANES)))
    sent = jnp.concatenate([early, late], axis=0)
    sent = jnp.broadcast_to(sent[None], (chips,) + sent.shape)
    mine = trade_chips(sent)
    updated, node_gradient = call(
        finish_kernel,
        [(node_block, BF), (node_block, F32)],
        returned, slot, cotangent, refined, grad_hidden, grad_sources, grad_targets, halo_lists, *halo_back,
        inner_weight, source_weight, target_weight,
        where=where,
    )
    shapes = [square, square, square, ((2 * width, width), F32), square, square]
    buffers = {"scratch": [((7 * width // 2, width), F32)], "sems": [(7,)], "far_out": 6, "where": where}
    results = call(results_kernel, shapes, mine, **buffers, early=early_rows, other=False)
    results = call(
        results_kernel, shapes, across(mine), *results, far_in=6, aliases=6,
        **buffers, early=early_rows, other=True,
    )
    return (updated, node_gradient, *results)


def solution(mesh):
    whole = mesh.devices.reshape(mesh.shape["row"] // 2, 2, -1, 4)
    mesh = Mesh(whole, ALL)
    in_specs = (
        P(ALL, None),
        P(ALL, None),
        P(ALL),
        P(ALL),
        P(ALL, None, None),
        P(ALL),
        P(ALL, None),
        P(),
        P(),
        P(),
        P(),
        P(),
        P(),
    )
    out_specs = (P(ALL, None), P(ALL, None), P(), P(), P(), P(), P(), P())

    return jax.shard_map(local, mesh=mesh, in_specs=in_specs, out_specs=out_specs, check_vma=False)
```

profile of v0, /device:TPU:1, one launch (start us, length us, event | category | flops | bytes accessed | tf_op | source)
XLA Modules:
  0.0 230.5 jit_solution(18411138635929436131)
XLA Ops:
  0.7 1.0 copy-done
  2.5 0.8 shard_map.188
  3.3 1.5 collective-permute-start
  4.8 3.6 %collective-permute-start.1 = (bf16[32,512]{1,0:T(8,128)(2,1)S(1)}, bf16[32,512]{1,0:T(8,128)(2,1)S(1)}, u32[]{:S(2)}, u32[]{:S(2)}) collective-permute-start(bf16[32,512]{1,0:T(8,128)(2,1)S(1)} %get-tuple-element.56), channel_id=1, source_target_pairs={{16,32},{48,64},{80,96},{32,16},{64,48},{96,80},{17,33},{49,65},{8... | collective-permute-start | bytes 98312 | tf_op jit(solution)/shard_map/ppermute | solution.py:358
  8.3 1.4 collective-permute-start.2
  10.4 1.0 copy-done.1
  11.4 1.0 copy-done.6
  12.4 1.0 copy-done.15
  14.2 0.8 shard_map.189
  15.4 1.0 copy-done.8
  16.4 1.0 copy-done.11
  17.5 1.0 copy-done.13
  18.5 11.5 %shard_map.190 = (bf16[2048,512]{1,0:T(8,128)(2,1)S(1)}, bf16[2048,512]{1,0:T(8,128)(2,1)S(1)}, bf16[2048,512]{1,0:T(8,128)(2,1)S(1)}, bf16[512,512]{1,0:T(8,128...) custom-call(s32[2]{0:T(128)S(1)} %pad_add_fusion.where, ...), custom_call_target="tpu_custom_call" | custom-call | tf_op jit(solution)/shard_map/pallas_call | solution.py:342
  30.0 1.3 copy-done.17
  31.3 1.3 copy-done.18
  32.7 1.3 copy-done.20
  34.0 1.3 copy-done.22
  35.3 0.8 copy-done.28
  36.1 0.8 copy-done.34
  36.9 0.8 copy-done.36
  37.7 0.8 copy-done.38
  38.5 11.3 %all-to-all-start = ((bf16[128,8,1024]{2,1,0:T(8,128)(2,1)}), bf16[128,8,1024]{2,1,0:T(8,128)(2,1)S(1)}, u32[]{:S(2)}, u32[]{:S(2)}) async-start(bf16[128,8,1024]{2,1,0:T(8,128)(2,1)} %bitcast.15), calls=%async_computation | async-start | bytes 4194304 | tf_op jit(solution)/shard_map/all_to_all | solution.py:371
  51.6 27.9 %all-to-all-done = bf16[128,8,1024]{2,1,0:T(8,128)(2,1)S(1)} async-done(((bf16[128,8,1024]{2,1,0:T(8,128)(2,1)}), bf16[128,8,1024]{2,1,0:T(8,128)(2,1)S(1)}, u32[]{:S(2)}, u32[]{:S(2)}) %all-to-all-start) | async-done | bytes 2097184 | tf_op jit(solution)/shard_map/all_to_all | solution.py:371
  79.5 1.0 copy-done.27
  80.6 0.9 copy-done.41
  81.5 0.8 copy-done.43
  82.4 1.4 shard_map.192
  83.9 34.0 %all_to_all.25 = bf16[128,8,1024]{2,1,0:T(8,128)(2,1)S(1)} all-to-all(bf16[128,8,1024]{2,1,0:T(8,128)(2,1)S(1)} %bitcast.16), channel_id=1, replica_groups=mesh['z'=4,'core'=2,'x'=4,'y'=4] {'z','core','x','y'}, dimensions={0} | all-to-all | bytes 4194304 | tf_op jit(solution)/shard_map/all_to_all | solution.py:371
  118.0 4.0 %shard_map.193 = (bf16[512,512]{1,0:T(8,128)(2,1)S(1)}, bf16[512,512]{1,0:T(8,128)(2,1)S(1)}, bf16[4096,128]{1,0:T(8,128)(2,1)S(1)}, bf16[4096,128]{1,0:T(8,128)(2,1)}) custom-call(s32[2]{0:T(128)S(1)} %copy-done.47, bf16[1024,1024]{1,0:T(8,128)(2,1)S(1)} %bitcast.12, s32[1,512]{1,0:T(1,128)S(1)} %copy-done.49, bf16[512,512]{1,0:T(8,128)(2,1)S(1)} %copy-done.9, ...), custom_call_target="tpu_custom_call" | custom-call | tf_op jit(solution)/shard_map/pallas_call | solution.py:342
  122.0 1.0 copy-done.24
  123.0 11.4 %shard_map.194 = (bf16[3072,128]{1,0:T(8,128)(2,1)S(1)}, bf16[3072,128]{1,0:T(8,128)(2,1)S(1)}, bf16[640,512]{1,0:T(8,128)(2,1)S(1)}, bf16[512,512]{1,0:T(8,128)...) custom-call(s32[2]{0:T(128)S(1)} %copy-done.47, ...), custom_call_target="tpu_custom_call" | custom-call | tf_op jit(solution)/shard_map/pallas_call | solution.py:342
  134.4 1.2 collective-permute-start.9
  135.7 1.8 collective-permute-done.9
  137.5 1.1 add_convert_fusion.1
  138.6 5.5 %all-to-all-start.3 = ((bf16[64,48,128]{2,1,0:T(8,128)(2,1)}), bf16[64,48,128]{2,1,0:T(8,128)(2,1)}, u32[]{:S(2)}, u32[]{:S(2)}) async-start(bf16[64,48,128]{2,1,0:T(8,128)(2,1)} %bitcast.24), calls=%async_computation.3 | async-start | bytes 1572864 | tf_op jit(solution)/shard_map/all_to_all | solution.py:384
  144.1 2.8 %add_convert_fusion = bf16[4096,128]{1,0:T(8,128)(2,1)} fusion(bf16[4096,128]{1,0:T(8,128)(2,1)} %collective-permute-done.8, bf16[4096,128]{1,0:T(8,128)(2,1)} %copy-done.24), kind=kLoop, calls=%fused_computation | loop fusion | flops 2097152 | bytes 3145728 | tf_op jit(solution)/shard_map/convert_element_type | solution.py:380
  146.9 12.3 %all-to-all-done.3 = bf16[64,48,128]{2,1,0:T(8,128)(2,1)} async-done(((bf16[64,48,128]{2,1,0:T(8,128)(2,1)}), bf16[64,48,128]{2,1,0:T(8,128)(2,1)}, u32[]{:S(2)}, u32[]{:S(2)}) %all-to-all-start.3) | async-done | bytes 786464 | tf_op jit(solution)/shard_map/all_to_all | solution.py:384
  159.2 5.7 %all-to-all-start.2 = ((bf16[64,64,128]{2,1,0:T(8,128)(2,1)}), bf16[64,64,128]{2,1,0:T(8,128)(2,1)}, u32[]{:S(2)}, u32[]{:S(2)}) async-start(bf16[64,64,128]{2,1,0:T(8,128)(2,1)} %bitcast.23), calls=%async_computation.2 | async-start | bytes 2097152 | tf_op jit(solution)/shard_map/all_to_all | solution.py:384
  165.0 1.3 reduce_sum.25
  166.3 15.1 %all-to-all-done.2 = bf16[64,64,128]{2,1,0:T(8,128)(2,1)} async-done(((bf16[64,64,128]{2,1,0:T(8,128)(2,1)}), bf16[64,64,128]{2,1,0:T(8,128)(2,1)}, u32[]{:S(2)}, u32[]{:S(2)}) %all-to-all-start.2) | async-done | bytes 1048608 | tf_op jit(solution)/shard_map/all_to_all | solution.py:384
  181.4 1.4 reduce_sum.24
  183.1 29.5 %all_to_all.26.gathered = bf16[64,112,128]{2,1,0:T(8,128)(2,1)S(1)} all-to-all(bf16[64,112,128]{2,1,0:T(8,128)(2,1)S(1)} %broadcast_in_dim.2), channel_id=1, replica_groups=mesh['z'=4,'core'=2,'x'=4,'y'=4] {'z','x','y'}, dimensions={0} | all-to-all | bytes 3670016 | tf_op jit(solution)/shard_map/all_to_all | solution.py:384
  212.6 3.4 %collective-permute-start.10 = (bf16[64,112,128]{2,1,0:T(8,128)(2,1)S(1)}, bf16[64,112,128]{2,1,0:T(8,128)(2,1)S(1)}, u32[]{:S(2)}, u32[]{:S(2)}) collective-permute-start(bf16[64,112,128]{2,1,0:T(8,128)(2,1)S(1)} %all_to_all.26.gathered), channel_id=1, source_target_pairs={{0,16},{16,0},{1,17},{17,1},{2,18},{18,2},{3,19},{19,3},{4,20},{20... | collective-permute-start | bytes 5505032 | tf_op jit(solution)/shard_map/ppermute | solution.py:376
  216.0 2.3 collective-permute-start.5
  219.5 1.8 collective-permute-done.5.back_1
  221.3 4.0 %shard_map.195 = (bf16[512,512]{1,0:T(8,128)(2,1)}, f32[512,512]{1,0:T(8,128)}) custom-call(s32[2]{0:T(128)S(1)} %copy-done.47, bf16[1024,1024]{1,0:T(8,128)(2,1)S(1)} %bitcast.13, s32[1,512]{1,0:T(1,128)S(1)} %copy-done.49, bf16[512,512]{1,0:T(8,128)(2,1)S(1)} %copy-done.10, bf16[512,512]{1,0:T(8,128)(2,1)S(1)} %copy-done.29, ...), custom_call_target="tpu_custom_call" | custom-call | tf_op jit(solution)/shard_map/pallas_call | solution.py:342
  225.3 2.5 %shard_map.196 = (f32[512,512]{1,0:T(8,128)}, f32[512,512]{1,0:T(8,128)}, f32[512,512]{1,0:T(8,128)}, f32[1024,512]{1,0:T(8,128)}, f32[512,512]{1,0:T(8,128)}, /*index=5*/f32[512,512]{1,0:T(8,128)}) custom-call(s32[2]{0:T(128)S(1)} %copy-done.47, bf16[64,112,128]{2,1,0:T(8,128)(2,1)S(1)} %all_to_all.26.gathered), custom_call_target="tpu_custom_call" | custom-call | tf_op jit(solution)/shard_map/pallas_call | solution.py:342
  227.8 2.5 %shard_map.197 = (f32[512,512]{1,0:T(8,128)}, f32[512,512]{1,0:T(8,128)}, f32[512,512]{1,0:T(8,128)}, f32[1024,512]{1,0:T(8,128)}, f32[512,512]{1,0:T(8,128)}, /*index=5*/f32[512,512]{1,0:T(8,128)}) custom-call(s32[2]{0:T(128)S(1)} %copy-done.47, ...), custom_call_target="tpu_custom_call", output_to_operand_aliasing={{0}: (2, {}), {1}: (3, {}), {2}: (4, {}), {3}: (5, {}), {4}... | custom-call | tf_op jit(solution)/shard_map/pallas_call | solution.py:342
  (107 shorter events, 5.9 us)
Async XLA Ops:
  0.6 14.4 %copy-start.45 = (s32[2048]{0:T(1024)S(1)}, s32[2048]{0:T(1024)}, u32[]{:S(2)}) copy-start(s32[2048]{0:T(1024)} %param.16) | copy-start | bytes 24580
  0.6 14.4 %copy-start.44 = (s32[2048]{0:T(1024)S(1)}, s32[2048]{0:T(1024)}, u32[]{:S(2)}) copy-start(s32[2048]{0:T(1024)} %param.15) | copy-start | bytes 24580
  2.5 27.5 %copy-start.46 = (s32[2]{0:T(128)}, s32[2]{0:T(128)S(1)}, u32[]{:S(2)}) copy-start(s32[2]{0:T(128)S(1)} %pad_add_fusion.where) | copy-start | bytes 28
  2.5 12.6 %copy-start.2 = (bf16[512,512]{1,0:T(8,128)(2,1)S(1)}, bf16[512,512]{1,0:T(8,128)(2,1)}, u32[]{:S(2)}) copy-start(bf16[512,512]{1,0:T(8,128)(2,1)} %nodes.9) | copy-start | bytes 1572868
  3.3 11.7 %collective-permute-start = (bf16[32,512]{1,0:T(8,128)(2,1)S(1)}, bf16[32,512]{1,0:T(8,128)(2,1)S(1)}, u32[]{:S(2)}, u32[]{:S(2)}) collective-permute-start(bf16[32,512]{1,0:T(8,128)(2,1)S(1)} %get-tuple-element.55), channel_id=1, source_target_pairs={{0,16},{32,48},{64,80},{96,112},{16,0},{48,32},{80,64},{112,96},{1... | collective-permute-start | bytes 98312 | tf_op jit(solution)/shard_map/ppermute | solution.py:358
  4.8 10.2 %collective-permute-start.1 = (bf16[32,512]{1,0:T(8,128)(2,1)S(1)}, bf16[32,512]{1,0:T(8,128)(2,1)S(1)}, u32[]{:S(2)}, u32[]{:S(2)}) collective-permute-start(bf16[32,512]{1,0:T(8,128)(2,1)S(1)} %get-tuple-element.56), channel_id=1, source_target_pairs={{16,32},{48,64},{80,96},{32,16},{64,48},{96,80},{17,33},{49,65},{8... | collective-permute-start | bytes 98312 | tf_op jit(solution)/shard_map/ppermute | solution.py:358
  8.3 6.7 %collective-permute-start.2 = (bf16[32,512]{1,0:T(8,128)(2,1)S(1)}, bf16[32,512]{1,0:T(8,128)(2,1)S(1)}, u32[]{:S(2)}, u32[]{:S(2)}) collective-permute-start(bf16[32,512]{1,0:T(8,128)(2,1)S(1)} %get-tuple-element.57), channel_id=1, source_target_pairs={{0,1},{2,3},{4,5},{6,7},{8,9},{10,11},{12,13},{14,15},{1,0},{3,2},... | collective-permute-start | bytes 98312 | tf_op jit(solution)/shard_map/ppermute | solution.py:358
  9.7 5.3 %collective-permute-start.3 = (bf16[32,512]{1,0:T(8,128)(2,1)S(1)}, bf16[32,512]{1,0:T(8,128)(2,1)S(1)}, u32[]{:S(2)}, u32[]{:S(2)}) collective-permute-start(bf16[32,512]{1,0:T(8,128)(2,1)S(1)} %get-tuple-element.58), channel_id=1, source_target_pairs={{1,2},{3,4},{5,6},{7,8},{9,10},{11,12},{13,14},{2,1},{4,3},{6,5},{... | collective-permute-start | bytes 98312 | tf_op jit(solution)/shard_map/ppermute | solution.py:358
  14.9 15.1 %copy-start.48 = (s32[1,512]{1,0:T(1,128)}, s32[1,512]{1,0:T(1,128)S(1)}, u32[]{:S(2)}) copy-start(s32[1,512]{1,0:T(1,128)S(1)} %get-tuple-element.61.slot) | copy-start | bytes 6148
  30.0 1.3 copy-start.17
  31.3 1.3 copy-start.18
  32.7 1.3 copy-start.20
  34.0 1.3 copy-start.22
  38.5 11.3 %copy-start.52 = (s32[1,1024]{1,0:T(1,128)S(1)}, s32[1,1024]{1,0:T(1,128)}, u32[]{:S(2)}) copy-start(s32[1,1024]{1,0:T(1,128)} %param.19) | copy-start | bytes 12292
  38.5 41.0 %all-to-all-start = ((bf16[128,8,1024]{2,1,0:T(8,128)(2,1)}), bf16[128,8,1024]{2,1,0:T(8,128)(2,1)S(1)}, u32[]{:S(2)}, u32[]{:S(2)}) async-start(bf16[128,8,1024]{2,1,0:T(8,128)(2,1)} %bitcast.15), calls=%async_computation | async-start | bytes 4194304 | tf_op jit(solution)/shard_map/all_to_all | solution.py:371
  82.4 35.6 %copy-start.35 = (bf16[512,512]{1,0:T(8,128)(2,1)S(1)}, bf16[512,512]{1,0:T(8,128)(2,1)}, u32[]{:S(2)}) copy-start(bf16[512,512]{1,0:T(8,128)(2,1)} %copy-done.34) | copy-start | bytes 1572868
  82.4 35.6 %copy-start.37 = (bf16[512,512]{1,0:T(8,128)(2,1)S(1)}, bf16[512,512]{1,0:T(8,128)(2,1)}, u32[]{:S(2)}) copy-start(bf16[512,512]{1,0:T(8,128)(2,1)} %copy-done.36) | copy-start | bytes 1572868
  82.4 35.6 %copy-start.39 = (bf16[512,512]{1,0:T(8,128)(2,1)S(1)}, bf16[512,512]{1,0:T(8,128)(2,1)}, u32[]{:S(2)}) copy-start(bf16[512,512]{1,0:T(8,128)(2,1)} %copy-done.38) | copy-start | bytes 1572868
  83.8 34.1 %copy-start.4 = (bf16[1024,512]{1,0:T(8,128)(2,1)S(1)}, bf16[1024,512]{1,0:T(8,128)(2,1)}, u32[]{:S(2)}) copy-start(bf16[1024,512]{1,0:T(8,128)(2,1)} %inner_weight.3) | copy-start | bytes 3145732
  83.8 34.1 %copy-start.9 = (bf16[512,512]{1,0:T(8,128)(2,1)S(1)}, bf16[512,512]{1,0:T(8,128)(2,1)}, u32[]{:S(2)}) copy-start(bf16[512,512]{1,0:T(8,128)(2,1)} %cotangent.5) | copy-start | bytes 1572868
  83.8 34.1 %copy-start.12 = (bf16[512,512]{1,0:T(8,128)(2,1)S(1)}, bf16[512,512]{1,0:T(8,128)(2,1)}, u32[]{:S(2)}) copy-start(bf16[512,512]{1,0:T(8,128)(2,1)} %outer_weight.1) | copy-start | bytes 1572868
  83.9 34.1 %copy-start.47 = (s32[2]{0:T(128)S(1)}, s32[2]{0:T(128)}, u32[]{:S(2)}) copy-start(s32[2]{0:T(128)} %copy-done.46) | copy-start | bytes 28
  83.9 34.1 %copy-start.49 = (s32[1,512]{1,0:T(1,128)S(1)}, s32[1,512]{1,0:T(1,128)}, u32[]{:S(2)}) copy-start(s32[1,512]{1,0:T(1,128)} %copy-done.48) | copy-start | bytes 6148
  83.9 39.1 %copy-start.23 = (bf16[2048,512]{1,0:T(8,128)(2,1)S(1)}, bf16[2048,512]{1,0:T(8,128)(2,1)}, u32[]{:S(2)}) copy-start(bf16[2048,512]{1,0:T(8,128)(2,1)} %copy-done.22) | copy-start | bytes 6291460
  118.0 5.0 %copy-start.7 = (bf16[512,512]{1,0:T(8,128)(2,1)S(1)}, bf16[512,512]{1,0:T(8,128)(2,1)}, u32[]{:S(2)}) copy-start(bf16[512,512]{1,0:T(8,128)(2,1)} %source_weight.7) | copy-start | bytes 1572868
  118.0 5.0 %copy-start.14 = (bf16[512,512]{1,0:T(8,128)(2,1)S(1)}, bf16[512,512]{1,0:T(8,128)(2,1)}, u32[]{:S(2)}) copy-start(bf16[512,512]{1,0:T(8,128)(2,1)} %edge_weight.3) | copy-start | bytes 1572868
  118.0 5.0 %copy-start.19 = (bf16[2048,512]{1,0:T(8,128)(2,1)S(1)}, bf16[2048,512]{1,0:T(8,128)(2,1)}, u32[]{:S(2)}) copy-start(bf16[2048,512]{1,0:T(8,128)(2,1)} %copy-done.18) | copy-start | bytes 6291460
  118.0 5.0 %copy-start.21 = (bf16[2048,512]{1,0:T(8,128)(2,1)S(1)}, bf16[2048,512]{1,0:T(8,128)(2,1)}, u32[]{:S(2)}) copy-start(bf16[2048,512]{1,0:T(8,128)(2,1)} %copy-done.20) | copy-start | bytes 6291460
  123.0 11.4 %copy-start.30 = (bf16[512,512]{1,0:T(8,128)(2,1)}, bf16[512,512]{1,0:T(8,128)(2,1)S(1)}, u32[]{:S(2)}) copy-start(bf16[512,512]{1,0:T(8,128)(2,1)S(1)} %get-tuple-element.73.grad_hidden) | copy-start | bytes 1572868
  134.4 4.2 %copy-start.25 = (bf16[640,512]{1,0:T(8,128)(2,1)}, bf16[640,512]{1,0:T(8,128)(2,1)S(1)}, u32[]{:S(2)}) copy-start(bf16[640,512]{1,0:T(8,128)(2,1)S(1)} %get-tuple-element.78.grad_sources) | copy-start | bytes 1966084
  134.4 4.2 %copy-start.32 = (bf16[512,512]{1,0:T(8,128)(2,1)}, bf16[512,512]{1,0:T(8,128)(2,1)S(1)}, u32[]{:S(2)}) copy-start(bf16[512,512]{1,0:T(8,128)(2,1)S(1)} %get-tuple-element.79.grad_targets) | copy-start | bytes 1572868
  134.4 3.1 %collective-permute-start.9 = (bf16[3072,128]{1,0:T(8,128)(2,1)S(1)}, bf16[3072,128]{1,0:T(8,128)(2,1)S(1)}, u32[]{:S(2)}, u32[]{:S(2)}) collective-permute-start(bf16[3072,128]{1,0:T(8,128)(2,1)S(1)} %get-tuple-element.89), channel_id=1, source_target_pairs={{0,16},{16,0},{1,17},{17,1},{2,18},{18,2},{3,19},{19,3},{4,20},{20... | collective-permute-start | bytes 2359304 | tf_op jit(solution)/shard_map/ppermute | solution.py:376
  135.6 8.5 %collective-permute-start.8 = (bf16[4096,128]{1,0:T(8,128)(2,1)}, bf16[4096,128]{1,0:T(8,128)(2,1)}, u32[]{:S(2)}, u32[]{:S(2)}) collective-permute-start(bf16[4096,128]{1,0:T(8,128)(2,1)} %get-tuple-element.87), channel_id=1, source_target_pairs={{0,16},{16,0},{1,17},{17,1},{2,18},{18,2},{3,19},{19,3},{4,20},{20... | collective-permute-start | bytes 3145736 | tf_op jit(solution)/shard_map/ppermute | solution.py:376
  138.6 20.6 %all-to-all-start.3 = ((bf16[64,48,128]{2,1,0:T(8,128)(2,1)}), bf16[64,48,128]{2,1,0:T(8,128)(2,1)}, u32[]{:S(2)}, u32[]{:S(2)}) async-start(bf16[64,48,128]{2,1,0:T(8,128)(2,1)} %bitcast.24), calls=%async_computation.3 | async-start | bytes 1572864 | tf_op jit(solution)/shard_map/all_to_all | solution.py:384
  159.2 22.1 %all-to-all-start.2 = ((bf16[64,64,128]{2,1,0:T(8,128)(2,1)}), bf16[64,64,128]{2,1,0:T(8,128)(2,1)}, u32[]{:S(2)}, u32[]{:S(2)}) async-start(bf16[64,64,128]{2,1,0:T(8,128)(2,1)} %bitcast.23), calls=%async_computation.2 | async-start | bytes 2097152 | tf_op jit(solution)/shard_map/all_to_all | solution.py:384
  182.8 38.5 %copy-start.31 = (bf16[512,512]{1,0:T(8,128)(2,1)S(1)}, bf16[512,512]{1,0:T(8,128)(2,1)}, u32[]{:S(2)}) copy-start(bf16[512,512]{1,0:T(8,128)(2,1)} %copy-done.30) | copy-start | bytes 1572868
  182.8 38.5 %copy-start.33 = (bf16[512,512]{1,0:T(8,128)(2,1)S(1)}, bf16[512,512]{1,0:T(8,128)(2,1)}, u32[]{:S(2)}) copy-start(bf16[512,512]{1,0:T(8,128)(2,1)} %copy-done.32) | copy-start | bytes 1572868
  183.1 38.2 %copy-start.5 = (bf16[1024,512]{1,0:T(8,128)(2,1)S(1)}, bf16[1024,512]{1,0:T(8,128)(2,1)}, u32[]{:S(2)}) copy-start(bf16[1024,512]{1,0:T(8,128)(2,1)} %inner_weight.3) | copy-start | bytes 3145732
  183.1 38.2 %copy-start.10 = (bf16[512,512]{1,0:T(8,128)(2,1)S(1)}, bf16[512,512]{1,0:T(8,128)(2,1)}, u32[]{:S(2)}) copy-start(bf16[512,512]{1,0:T(8,128)(2,1)} %cotangent.5) | copy-start | bytes 1572868
  183.1 38.2 %copy-start.16 = (bf16[512,512]{1,0:T(8,128)(2,1)S(1)}, bf16[512,512]{1,0:T(8,128)(2,1)}, u32[]{:S(2)}) copy-start(bf16[512,512]{1,0:T(8,128)(2,1)} %target_weight.3) | copy-start | bytes 1572868
  183.1 38.2 %copy-start.26 = (bf16[640,512]{1,0:T(8,128)(2,1)S(1)}, bf16[640,512]{1,0:T(8,128)(2,1)}, u32[]{:S(2)}) copy-start(bf16[640,512]{1,0:T(8,128)(2,1)} %copy-done.25) | copy-start | bytes 1966084
  183.1 38.2 %copy-start.29 = (bf16[512,512]{1,0:T(8,128)(2,1)S(1)}, bf16[512,512]{1,0:T(8,128)(2,1)}, u32[]{:S(2)}) copy-start(bf16[512,512]{1,0:T(8,128)(2,1)} %copy-done.28) | copy-start | bytes 1572868
  183.1 38.2 %copy-start.51 = (s32[1,4,32]{2,1,0:T(4,128)S(1)}, s32[1,4,32]{2,1,0:T(4,128)}, u32[]{:S(2)}) copy-start(s32[1,4,32]{2,1,0:T(4,128)} %lists.3) | copy-start | bytes 1540
  212.6 15.2 %collective-permute-start.10 = (bf16[64,112,128]{2,1,0:T(8,128)(2,1)S(1)}, bf16[64,112,128]{2,1,0:T(8,128)(2,1)S(1)}, u32[]{:S(2)}, u32[]{:S(2)}) collective-permute-start(bf16[64,112,128]{2,1,0:T(8,128)(2,1)S(1)} %all_to_all.26.gathered), channel_id=1, source_target_pairs={{0,16},{16,0},{1,17},{17,1},{2,18},{18,2},{3,19},{19,3},{4,20},{20... | collective-permute-start | bytes 5505032 | tf_op jit(solution)/shard_map/ppermute | solution.py:376
  216.0 3.5 %collective-permute-start.4 = (bf16[32,512]{1,0:T(8,128)(2,1)S(1)}, bf16[32,512]{1,0:T(8,128)(2,1)S(1)}, u32[]{:S(2)}, u32[]{:S(2)}) collective-permute-start(bf16[32,512]{1,0:T(8,128)(2,1)S(1)} %get-tuple-element.80), channel_id=1, source_target_pairs={{0,16},{32,48},{64,80},{96,112},{16,0},{48,32},{80,64},{112,96},{1... | collective-permute-start | bytes 98312 | tf_op jit(solution)/shard_map/ppermute | solution.py:358
  216.0 5.2 %collective-permute-start.5 = (bf16[32,512]{1,0:T(8,128)(2,1)S(1)}, bf16[32,512]{1,0:T(8,128)(2,1)S(1)}, u32[]{:S(2)}, u32[]{:S(2)}) collective-permute-start(bf16[32,512]{1,0:T(8,128)(2,1)S(1)} %get-tuple-element.81), channel_id=1, source_target_pairs={{16,32},{48,64},{80,96},{32,16},{64,48},{96,80},{17,33},{49,65},{8... | collective-permute-start | bytes 98312 | tf_op jit(solution)/shard_map/ppermute | solution.py:358
  218.3 2.9 %collective-permute-start.6 = (bf16[32,512]{1,0:T(8,128)(2,1)S(1)}, bf16[32,512]{1,0:T(8,128)(2,1)S(1)}, u32[]{:S(2)}, u32[]{:S(2)}) collective-permute-start(bf16[32,512]{1,0:T(8,128)(2,1)S(1)} %get-tuple-element.82), channel_id=1, source_target_pairs={{0,1},{2,3},{4,5},{6,7},{8,9},{10,11},{12,13},{14,15},{1,0},{3,2},... | collective-permute-start | bytes 98312 | tf_op jit(solution)/shard_map/ppermute | solution.py:358
  218.7 2.5 %collective-permute-start.7 = (bf16[32,512]{1,0:T(8,128)(2,1)S(1)}, bf16[32,512]{1,0:T(8,128)(2,1)S(1)}, u32[]{:S(2)}, u32[]{:S(2)}) collective-permute-start(bf16[32,512]{1,0:T(8,128)(2,1)S(1)} %get-tuple-element.83), channel_id=1, source_target_pairs={{1,2},{3,4},{5,6},{7,8},{9,10},{11,12},{13,14},{2,1},{4,3},{6,5},{... | collective-permute-start | bytes 98312 | tf_op jit(solution)/shard_map/ppermute | solution.py:358
  (20 other events, 18.2 us)
where the time goes:
time: 235 us; the launch traced here: 230 us
  blocking collectives  63.5 us (27%)
  waiting for transfers between devices  59.1 us (25%)
  Pallas kernels  39.3 us (17%)
  starting transfers between devices  37.6 us (16%)
  local copies, waits for them, and re-layouts  23 us (10%)
  other arithmetic  6.63 us (3%)
    pallas_call x10, Pallas kernels, call(): pl.pallas_call(body, in_specs=specs, out_specs=[far] * far_out + [near] *...  39.3 us
    all_to_all x1, blocking collectives, trade_slots(): moved = lax.all_to_all(shaped, ALL, split_axis=0, concat_axis=0, tiled=True)  34 us
    all_to_all x1, blocking collectives, trade_chips(): return lax.all_to_all(value, CHIPS, split_axis=0, concat_axis=0, tiled=True)  29.5 us
    all_to_all x1, waiting for transfers between devices, trade_slots(): moved = lax.all_to_all(shaped, ALL, split_axis=0, concat_axis=0, tiled=True)  27.9 us
    all_to_all x2, waiting for transfers between devices, trade_chips(): return lax.all_to_all(value, CHIPS, split_axis=0, concat_axis=0, tiled=True)  27.4 us
    unnamed x108, local copies, waits for them, and re-layouts  22.8 us
    all_to_all x1, starting transfers between devices, trade_slots(): moved = lax.all_to_all(shaped, ALL, split_axis=0, concat_axis=0, tiled=True)  11.3 us
    all_to_all x2, starting transfers between devices, trade_chips(): return lax.all_to_all(value, CHIPS, split_axis=0, concat_axis=0, tiled=True)  11.2 us
  transfers between devices with their start and end apart: 14, of which 6 were waited for; matrix products, arithmetic and copies ran while one was open for 2% of the time, Pallas kernels for 3%

commit v1 on v0

--- a/solution.py
+++ b/solution.py
@@ -14,6 +14,8 @@
 F32 = jnp.float32
 LANES = 128
 CHUNK = 1024
+SMALL = 32
+LARGE = 60
 CAPACITY = 8
 ROW = ("z", "core")
 COL = ("x", "y")
@@ -172,29 +174,21 @@
         store.wait()
 
 
-def members_kernel(table, members, picks, counts):
-    coarse = members.shape[0]
+def coarse_kernel(arrived, table, weight, out, coarse_out, grad_out):
+    rows, width = coarse_out.shape
     row = wide_row(table)
-    inside = iota((coarse, row.shape[1]), 0) == row
-    ones = jnp.where(inside, 1.0, 0.0)
-    members[...] = ones.astype(BF)
-    count = jnp.maximum(jnp.sum(ones, axis=1, keepdims=True), 1.0)
-    counts[...] = jnp.broadcast_to(count, counts.shape)
-    picks[...] = hot(wide_column(row) == iota((row.shape[1], coarse), 1))
-
-
-def coarse_kernel(arrived, members, picks, counts, weight, out, coarse_out, grad_out):
-    width = weight.shape[0]
-    count = counts[:, :1]
-    totals = dot(members[...], arrived[...])
+    members = jnp.where(iota((rows, row.shape[1]), 0) == row, 1.0, 0.0)
+    count = jnp.maximum(jnp.sum(members, axis=1, keepdims=True), 1.0)
+    picks = hot(wide_column(row) == iota((row.shape[1], rows), 1))
+    totals = dot(members.astype(BF), arrived[...])
     coarse = (totals[:, :width] / count).astype(BF)
     coarse_out[...] = coarse
     active, slope = gates(dot(coarse, weight[...]))
     grad = (totals[:, width:] * slope).astype(BF)
     grad_out[...] = grad
     share = (right_dot(grad, weight[...]) / count).astype(BF)
-    out[:, :width] = dot(picks[...], share).astype(BF)
-    out[:, width:] = dot(picks[...], active.astype(BF)).astype(BF)
+    out[:, :width] = dot(picks, share).astype(BF)
+    out[:, width:] = dot(picks, active.astype(BF)).astype(BF)
 
 
 def half_of(ref, half):
@@ -333,7 +327,7 @@
         store.wait()
 
 
-def call(kernel, outs, *args, far_in=0, far_out=0, scratch=(), sems=(), where=None, aliases=0, **static):
+def call(kernel, outs, *args, far_in=0, far_out=0, scratch=(), sems=(), where=None, aliases=0, grant=LARGE, **static):
     body = functools.partial(kernel, *static.values())
     near, far = pl.BlockSpec(memory_space=pltpu.VMEM), pl.BlockSpec(memory_space=pl.ANY)
     specs = [near] * (len(args) - far_in) + [far] * far_in
@@ -346,7 +340,7 @@
         out_shape=[jax.ShapeDtypeStruct(shape, dtype) for shape, dtype in outs],
         scratch_shapes=[pltpu.VMEM(shape, dtype) for shape, dtype in scratch]
         + [pltpu.SemaphoreType.DMA(shape) for shape in sems],
-        compiler_params=pltpu.CompilerParams(vmem_limit_bytes=32 * 2 ** 20),
+        compiler_params=pltpu.CompilerParams(vmem_limit_bytes=grant * 2 ** 20),
         input_output_aliases={len(args) - aliases + k: k for k in range(aliases)},
     )(*args)
 
@@ -440,15 +434,11 @@
         where=where,
     )
     arrived = trade_slots(sent, devices)
-    members, picks, counts = call(
-        members_kernel,
-        [((coarse_rows, slots), BF), ((slots, coarse_rows), BF), ((coarse_rows, LANES), F32)],
-        table,
-    )
     sent, coarse, grad_coarse = call(
         coarse_kernel,
         [((slots, 2 * width), BF)] + [((coarse_rows, width), BF)] * 2,
-        arrived, members, picks, counts, coarse_weight,
+        arrived, table, coarse_weight,
+        grant=SMALL,
     )
     returned = trade_slots(sent, devices)
     grad_aggregate, grad_hidden, keep, give = call(
@@ -456,7 +446,7 @@
         [(node_block, BF), (node_block, BF), ((4 * packed, LANES), BF), ((4 * packed, LANES), BF)],
         returned, slot, cotangent, nodes, aggregate, node_hidden, node_slope, coarse, grad_coarse,
         inner_weight, outer_weight,
-        where=where, scale=scale,
+        where=where, grant=SMALL, scale=scale,
     )
     early = paired(keep, give)
     early_rows = 4 * packed // chips
@@ -486,7 +476,7 @@
         where=where,
     )
     shapes = [square, square, square, ((2 * width, width), F32), square, square]
-    buffers = {"scratch": [((7 * width // 2, width), F32)], "sems": [(7,)], "far_out": 6, "where": where}
+    buffers = {"scratch": [((7 * width // 2, width), F32)], "sems": [(7,)], "far_out": 6, "where": where, "grant": SMALL}
     results = call(results_kernel, shapes, mine, **buffers, early=early_rows, other=False)
     results = call(
         results_kernel, shapes, across(mine), *results, far_in=6, aliases=6,

time: 235 us -> 226 us (0.962)
  blocking collectives: 63.5 us -> 106 us
  waiting for transfers between devices: 59.1 us -> 32.3 us
  local copies, waits for them, and re-layouts: 23 us -> 5.07 us
  starting transfers between devices: 37.6 us -> 24.8 us
  Pallas kernels: 39.3 us -> 47.2 us
    all_to_all x1 -> x2, blocking collectives: 34 us -> 76.7 us  [trade_slots(): moved = lax.all_to_all(shaped, ALL, split_axis=0, concat_axis=0, tiled=True)]
    all_to_all x1 -> x0, waiting for transfers between devices: 27.9 us -> none  [trade_slots(): moved = lax.all_to_all(shaped, ALL, split_axis=0, concat_axis=0, tiled=True)]
    unnamed x108 -> x62, local copies, waits for them, and re-layouts: 22.8 us -> 4.83 us
    all_to_all x1 -> x0, starting transfers between devices: 11.3 us -> none  [trade_slots(): moved = lax.all_to_all(shaped, ALL, split_axis=0, concat_axis=0, tiled=True)]
    pallas_call x10 -> x9, Pallas kernels: 39.3 us -> 47.2 us  [call(): pl.pallas_call(body, in_specs=specs, out_specs=[far] * far_out + [near] *...]
    reduce_sum x2, other arithmetic: 2.68 us -> 0.32 us  [total(): return jnp.sum(arrived.astype(F32), axis=0).astype(BF)]
  transfers between devices with their start and end apart: 14 -> 13, of which waited for: 6 -> 5; matrix products, arithmetic and copies ran while one was open for 2% -> 2% of each run, Pallas kernels for 3% -> 5%
where the time goes in v1:
time: 226 us; the launch traced here: 222 us
  blocking collectives  106 us (47%)
  Pallas kernels  47.2 us (21%)
  waiting for transfers between devices  32.3 us (14%)
  starting transfers between devices  24.8 us (11%)
  other arithmetic  5.65 us (2%)
  local copies, waits for them, and re-layouts  5.07 us (2%)
    all_to_all x2, blocking collectives, trade_slots(): moved = lax.all_to_all(shaped, ALL, split_axis=0, concat_axis=0, tiled=True)  76.7 us
    pallas_call x9, Pallas kernels, call(): pl.pallas_call(body, in_specs=specs, out_specs=[far] * far_out + [near] *...  47.2 us
    all_to_all x1, blocking collectives, trade_chips(): return lax.all_to_all(value, CHIPS, split_axis=0, concat_axis=0, tiled=True)  29.2 us
    all_to_all x2, waiting for transfers between devices, trade_chips(): return lax.all_to_all(value, CHIPS, split_axis=0, concat_axis=0, tiled=True)  28.4 us
    ppermute x8, starting transfers between devices, swapped(): return lax.ppermute(value, axis, pairs)  10.3 us
    all_to_all x2, starting transfers between devices, trade_chips(): return lax.all_to_all(value, CHIPS, split_axis=0, concat_axis=0, tiled=True)  9.65 us
    ppermute x3, starting transfers between devices, across(): return lax.ppermute(value, 'core', [(0, 1), (1, 0)])  4.88 us
    unnamed x62, local copies, waits for them, and re-layouts  4.83 us
  transfers between devices with their start and end apart: 13, of which 5 were waited for; matrix products, arithmetic and copies ran while one was open for 2% of the time, Pallas kernels for 5%

profile of v1, /device:TPU:1, one launch (start us, length us, event | category | flops | bytes accessed | tf_op | source)
XLA Modules:
  0.0 222.2 jit_solution(10023342030928041764)
XLA Ops:
  0.6 0.6 pad_add_fusion.where
  1.3 2.0 shard_map.188
  3.2 1.4 collective-permute-start
  4.6 3.5 %collective-permute-start.1 = (bf16[32,512]{1,0:T(8,128)(2,1)}, bf16[32,512]{1,0:T(8,128)(2,1)S(1)}, u32[]{:S(2)}, u32[]{:S(2)}) collective-permute-start(bf16[32,512]{1,0:T(8,128)(2,1)} %get-tuple-element.53), channel_id=1, source_target_pairs={{16,32},{48,64},{80,96},{32,16},{64,48},{96,80},{17,33},{49,65},{8... | collective-permute-start | bytes 98312 | tf_op jit(solution)/shard_map/ppermute | solution.py:352
  8.2 1.4 collective-permute-start.2
  9.5 0.7 collective-permute-start.3
  10.2 2.9 %shard_map.189 = (s32[1,512]{1,0:T(1,128)}, bf16[512,512]{1,0:T(8,128)(2,1)}, bf16[512,512]{1,0:T(8,128)(2,1)}) custom-call(s32[4,128]{1,0:T(4,128)} %bitcast.23, bf16[512,512]{1,0:T(8,128)(2,1)} %nodes.9, bf16[512,512]{1,0:T(8,128)(2,1)} %source_weight.7, bf16[512,512]{1,0:T(8,128)(2,1)} %target_weight.3), custom_call_target="tpu_custom_call" | custom-call | tf_op jit(solution)/shard_map/pallas_call | solution.py:336
  13.2 0.6 copy-done.19
  13.8 0.0 copy-done.21
  13.8 0.0 copy-done.22
  13.8 13.0 %shard_map.190 = (bf16[2048,512]{1,0:T(8,128)(2,1)}, bf16[2048,512]{1,0:T(8,128)(2,1)}, bf16[2048,512]{1,0:T(8,128)(2,1)}, bf16[512,512]{1,0:T(8,128)(2,1)}, bf1...) custom-call(s32[2]{0:T(128)} %pad_add_fusion.where, ...), custom_call_target="tpu_custom_call" | custom-call | tf_op jit(solution)/shard_map/pallas_call | solution.py:336
  26.8 0.0 copy-start.16
  26.8 42.5 %all_to_all.25 = bf16[128,8,1024]{2,1,0:T(8,128)(2,1)S(1)} all-to-all(bf16[128,8,1024]{2,1,0:T(8,128)(2,1)} %bitcast.18), channel_id=1, replica_groups=mesh['z'=4,'core'=2,'x'=4,'y'=4] {'z','core','x','y'}, dimensions={0} | all-to-all | bytes 4194304 | tf_op jit(solution)/shard_map/all_to_all | solution.py:365
  69.3 1.5 shard_map.191
  70.8 0.0 copy-start.3
  70.9 0.0 copy-start.4
  70.9 34.2 %all_to_all.26 = bf16[128,8,1024]{2,1,0:T(8,128)(2,1)S(1)} all-to-all(bf16[128,8,1024]{2,1,0:T(8,128)(2,1)S(1)} %bitcast.15), channel_id=1, replica_groups=mesh['z'=4,'core'=2,'x'=4,'y'=4] {'z','core','x','y'}, dimensions={0} | all-to-all | bytes 4194304 | tf_op jit(solution)/shard_map/all_to_all | solution.py:365
  105.2 3.0 %shard_map.192 = (bf16[512,512]{1,0:T(8,128)(2,1)S(1)}, bf16[512,512]{1,0:T(8,128)(2,1)S(1)}, bf16[4096,128]{1,0:T(8,128)(2,1)S(1)}, bf16[4096,128]{1,0:T(8,128)(2,1)S(1)}) custom-call(s32[2]{0:T(128)S(1)} %copy-done.13, bf16[1024,1024]{1,0:T(8,128)(2,1)S(1)} %bitcast.12, s32[1,512]{1,0:T(1,128)S(1)} %copy-done.15, bf16[512,512]{1,0:T(8,128)(2,1)S(1)} %copy-done.3, ...), custom_call_target="tpu_custom_call" | custom-call | tf_op jit(solution)/shard_map/pallas_call | solution.py:336
  108.3 1.0 copy-done.5
  109.2 0.8 copy-done.8
  110.0 0.8 copy-done.9
  110.8 1.0 copy-done.17
  111.8 13.3 %shard_map.193 = (bf16[3072,128]{1,0:T(8,128)(2,1)}, bf16[3072,128]{1,0:T(8,128)(2,1)}, bf16[640,512]{1,0:T(8,128)(2,1)}, bf16[512,512]{1,0:T(8,128)(2,1)}, bf16...) custom-call(s32[2]{0:T(128)} %pad_add_fusion.where, ...), custom_call_target="tpu_custom_call" | custom-call | tf_op jit(solution)/shard_map/pallas_call | solution.py:336
  125.1 1.2 collective-permute-start.9
  126.3 0.1 collective-permute-start.8
  126.4 2.0 collective-permute-done.9
  128.4 2.2 add_convert_fusion.1
  130.6 4.9 %all-to-all-start.3 = ((bf16[64,48,128]{2,1,0:T(8,128)(2,1)}), bf16[64,48,128]{2,1,0:T(8,128)(2,1)S(1)}, u32[]{:S(2)}, u32[]{:S(2)}) async-start(bf16[64,48,128]{2,1,0:T(8,128)(2,1)} %bitcast.17), calls=%async_computation.3 | async-start | bytes 1572864 | tf_op jit(solution)/shard_map/all_to_all | solution.py:378
  135.5 2.5 %add_convert_fusion = bf16[4096,128]{1,0:T(8,128)(2,1)} fusion(bf16[4096,128]{1,0:T(8,128)(2,1)} %collective-permute-done.8, bf16[4096,128]{1,0:T(8,128)(2,1)S(1)} %copy-done.6), kind=kLoop, calls=%fused_computation | loop fusion | flops 2097152 | bytes 3145728 | tf_op jit(solution)/shard_map/convert_element_type | solution.py:374
  138.0 12.3 %all-to-all-done.3 = bf16[64,48,128]{2,1,0:T(8,128)(2,1)S(1)} async-done(((bf16[64,48,128]{2,1,0:T(8,128)(2,1)}), bf16[64,48,128]{2,1,0:T(8,128)(2,1)S(1)}, u32[]{:S(2)}, u32[]{:S(2)}) %all-to-all-start.3) | async-done | bytes 786464 | tf_op jit(solution)/shard_map/all_to_all | solution.py:378
  150.3 4.8 %all-to-all-start.2 = ((bf16[64,64,128]{2,1,0:T(8,128)(2,1)}), bf16[64,64,128]{2,1,0:T(8,128)(2,1)S(1)}, u32[]{:S(2)}, u32[]{:S(2)}) async-start(bf16[64,64,128]{2,1,0:T(8,128)(2,1)} %bitcast.10), calls=%async_computation.2 | async-start | bytes 2097152 | tf_op jit(solution)/shard_map/all_to_all | solution.py:378
  155.1 0.1 reduce_sum.25
  155.2 16.1 %all-to-all-done.2 = bf16[64,64,128]{2,1,0:T(8,128)(2,1)S(1)} async-done(((bf16[64,64,128]{2,1,0:T(8,128)(2,1)}), bf16[64,64,128]{2,1,0:T(8,128)(2,1)S(1)}, u32[]{:S(2)}, u32[]{:S(2)}) %all-to-all-start.2) | async-done | bytes 1048608 | tf_op jit(solution)/shard_map/all_to_all | solution.py:378
  171.3 0.2 reduce_sum.24
  171.5 0.2 broadcast_in_dim.2
  171.8 29.2 %all_to_all.27.gathered = bf16[64,112,128]{2,1,0:T(8,128)(2,1)S(1)} all-to-all(bf16[64,112,128]{2,1,0:T(8,128)(2,1)S(1)} %broadcast_in_dim.2), channel_id=1, replica_groups=mesh['z'=4,'core'=2,'x'=4,'y'=4] {'z','x','y'}, dimensions={0} | all-to-all | bytes 3670016 | tf_op jit(solution)/shard_map/all_to_all | solution.py:378
  201.0 3.6 %collective-permute-start.10 = (bf16[64,112,128]{2,1,0:T(8,128)(2,1)S(1)}, bf16[64,112,128]{2,1,0:T(8,128)(2,1)S(1)}, u32[]{:S(2)}, u32[]{:S(2)}) collective-permute-start(bf16[64,112,128]{2,1,0:T(8,128)(2,1)S(1)} %all_to_all.27.gathered), channel_id=1, source_target_pairs={{0,16},{16,0},{1,17},{17,1},{2,18},{18,2},{3,19},{19,3},{4,20},{20... | collective-permute-start | bytes 5505032 | tf_op jit(solution)/shard_map/ppermute | solution.py:370
  204.6 2.3 %collective-permute-start.5 = (bf16[32,512]{1,0:T(8,128)(2,1)S(1)}, bf16[32,512]{1,0:T(8,128)(2,1)S(1)}, u32[]{:S(2)}, u32[]{:S(2)}) collective-permute-start(bf16[32,512]{1,0:T(8,128)(2,1)S(1)} %copy-done.29), channel_id=1, source_target_pairs={{16,32},{48,64},{80,96},{32,16},{64,48},{96,80},{17,33},{49,65},{8... | collective-permute-start | bytes 98312 | tf_op jit(solution)/shard_map/ppermute | solution.py:352
  206.9 0.4 collective-permute-start.6
  207.4 0.7 collective-permute-start.7
  208.0 0.1 collective-permute-done.4.back_0
  208.1 1.8 collective-permute-done.5.back_1
  209.9 0.6 copy-done.24
  210.5 0.0 copy-done.25
  210.5 0.0 copy-done.26
  210.5 6.5 %shard_map.194 = (bf16[512,512]{1,0:T(8,128)(2,1)}, f32[512,512]{1,0:T(8,128)}) custom-call(s32[2]{0:T(128)} %pad_add_fusion.where, bf16[1024,1024]{1,0:T(8,128)(2,1)} %bitcast.13, s32[1,512]{1,0:T(1,128)} %get-tuple-element.58.slot, bf16[512,512]{1,0:T(8,128)(2,1)} %cotangent.5, bf16[512,512]{1,0:T(8,128)(2,1)} %get-tuple-element.61.refined, ...), custom_call_target="tpu_custom_call" | custom-call | tf_op jit(solution)/shard_map/pallas_call | solution.py:336
  217.0 2.5 %shard_map.195 = (f32[512,512]{1,0:T(8,128)}, f32[512,512]{1,0:T(8,128)}, f32[512,512]{1,0:T(8,128)}, f32[1024,512]{1,0:T(8,128)}, f32[512,512]{1,0:T(8,128)}, /*index=5*/f32[512,512]{1,0:T(8,128)}) custom-call(s32[2]{0:T(128)S(1)} %copy-done.14, bf16[64,112,128]{2,1,0:T(8,128)(2,1)S(1)} %all_to_all.27.gathered), custom_call_target="tpu_custom_call" | custom-call | tf_op jit(solution)/shard_map/pallas_call | solution.py:336
  219.5 2.5 %shard_map.196 = (f32[512,512]{1,0:T(8,128)}, f32[512,512]{1,0:T(8,128)}, f32[512,512]{1,0:T(8,128)}, f32[1024,512]{1,0:T(8,128)}, f32[512,512]{1,0:T(8,128)}, /*index=5*/f32[512,512]{1,0:T(8,128)}) custom-call(s32[2]{0:T(128)S(1)} %copy-done.14, ...), custom_call_target="tpu_custom_call", output_to_operand_aliasing={{0}: (2, {}), {1}: (3, {}), {2}: (4, {}), {3}: (5, {}), {4}... | custom-call | tf_op jit(solution)/shard_map/pallas_call | solution.py:336
  (59 shorter events, 0.1 us)
Async XLA Ops:
  3.2 9.9 %collective-permute-start = (bf16[32,512]{1,0:T(8,128)(2,1)}, bf16[32,512]{1,0:T(8,128)(2,1)S(1)}, u32[]{:S(2)}, u32[]{:S(2)}) collective-permute-start(bf16[32,512]{1,0:T(8,128)(2,1)} %get-tuple-element.52), channel_id=1, source_target_pairs={{0,16},{32,48},{64,80},{96,112},{16,0},{48,32},{80,64},{112,96},{1... | collective-permute-start | bytes 98312 | tf_op jit(solution)/shard_map/ppermute | solution.py:352
  4.6 8.5 %collective-permute-start.1 = (bf16[32,512]{1,0:T(8,128)(2,1)}, bf16[32,512]{1,0:T(8,128)(2,1)S(1)}, u32[]{:S(2)}, u32[]{:S(2)}) collective-permute-start(bf16[32,512]{1,0:T(8,128)(2,1)} %get-tuple-element.53), channel_id=1, source_target_pairs={{16,32},{48,64},{80,96},{32,16},{64,48},{96,80},{17,33},{49,65},{8... | collective-permute-start | bytes 98312 | tf_op jit(solution)/shard_map/ppermute | solution.py:352
  8.2 5.0 %collective-permute-start.2 = (bf16[32,512]{1,0:T(8,128)(2,1)}, bf16[32,512]{1,0:T(8,128)(2,1)S(1)}, u32[]{:S(2)}, u32[]{:S(2)}) collective-permute-start(bf16[32,512]{1,0:T(8,128)(2,1)} %get-tuple-element.54), channel_id=1, source_target_pairs={{0,1},{2,3},{4,5},{6,7},{8,9},{10,11},{12,13},{14,15},{1,0},{3,2},... | collective-permute-start | bytes 98312 | tf_op jit(solution)/shard_map/ppermute | solution.py:352
  9.5 3.6 %collective-permute-start.3 = (bf16[32,512]{1,0:T(8,128)(2,1)}, bf16[32,512]{1,0:T(8,128)(2,1)S(1)}, u32[]{:S(2)}, u32[]{:S(2)}) collective-permute-start(bf16[32,512]{1,0:T(8,128)(2,1)} %get-tuple-element.55), channel_id=1, source_target_pairs={{1,2},{3,4},{5,6},{7,8},{9,10},{11,12},{13,14},{2,1},{4,3},{6,5},{... | collective-permute-start | bytes 98312 | tf_op jit(solution)/shard_map/ppermute | solution.py:352
  13.1 0.6 copy-start.19
  13.2 0.6 copy-start.20
  13.2 0.6 copy-start.21
  13.2 0.6 copy-start.22
  26.8 42.5 %copy-start.7 = (bf16[512,512]{1,0:T(8,128)(2,1)S(1)}, bf16[512,512]{1,0:T(8,128)(2,1)}, u32[]{:S(2)}) copy-start(bf16[512,512]{1,0:T(8,128)(2,1)} %weight.1) | copy-start | bytes 1572868
  26.8 42.5 %copy-start.16 = (s32[1,1024]{1,0:T(1,128)S(1)}, s32[1,1024]{1,0:T(1,128)}, u32[]{:S(2)}) copy-start(s32[1,1024]{1,0:T(1,128)} %param.19) | copy-start | bytes 12292
  70.8 34.3 %copy-start.1 = (bf16[512,512]{1,0:T(8,128)(2,1)S(1)}, bf16[512,512]{1,0:T(8,128)(2,1)}, u32[]{:S(2)}) copy-start(bf16[512,512]{1,0:T(8,128)(2,1)} %nodes.9) | copy-start | bytes 1572868
  70.8 34.3 %copy-start.2 = (bf16[1024,512]{1,0:T(8,128)(2,1)S(1)}, bf16[1024,512]{1,0:T(8,128)(2,1)}, u32[]{:S(2)}) copy-start(bf16[1024,512]{1,0:T(8,128)(2,1)} %inner_weight.3) | copy-start | bytes 3145732
  70.8 34.3 %copy-start.3 = (bf16[512,512]{1,0:T(8,128)(2,1)S(1)}, bf16[512,512]{1,0:T(8,128)(2,1)}, u32[]{:S(2)}) copy-start(bf16[512,512]{1,0:T(8,128)(2,1)} %cotangent.5) | copy-start | bytes 1572868
  70.9 34.3 %copy-start.4 = (bf16[512,512]{1,0:T(8,128)(2,1)S(1)}, bf16[512,512]{1,0:T(8,128)(2,1)}, u32[]{:S(2)}) copy-start(bf16[512,512]{1,0:T(8,128)(2,1)} %outer_weight.1) | copy-start | bytes 1572868
  70.9 34.3 %copy-start.10 = (bf16[512,512]{1,0:T(8,128)(2,1)S(1)}, bf16[512,512]{1,0:T(8,128)(2,1)}, u32[]{:S(2)}) copy-start(bf16[512,512]{1,0:T(8,128)(2,1)} %get-tuple-element.62.aggregate) | copy-start | bytes 1572868
  70.9 34.3 %copy-start.11 = (bf16[512,512]{1,0:T(8,128)(2,1)S(1)}, bf16[512,512]{1,0:T(8,128)(2,1)}, u32[]{:S(2)}) copy-start(bf16[512,512]{1,0:T(8,128)(2,1)} %get-tuple-element.63.node_hidden) | copy-start | bytes 1572868
  70.9 34.3 %copy-start.12 = (bf16[512,512]{1,0:T(8,128)(2,1)S(1)}, bf16[512,512]{1,0:T(8,128)(2,1)}, u32[]{:S(2)}) copy-start(bf16[512,512]{1,0:T(8,128)(2,1)} %get-tuple-element.64.node_slope) | copy-start | bytes 1572868
  70.9 34.3 %copy-start.13 = (s32[2]{0:T(128)S(1)}, s32[2]{0:T(128)}, u32[]{:S(2)}) copy-start(s32[2]{0:T(128)} %pad_add_fusion.where) | copy-start | bytes 28
  70.9 34.3 %copy-start.15 = (s32[1,512]{1,0:T(1,128)S(1)}, s32[1,512]{1,0:T(1,128)}, u32[]{:S(2)}) copy-start(s32[1,512]{1,0:T(1,128)} %get-tuple-element.58.slot) | copy-start | bytes 6148
  105.1 3.1 %copy-start = (bf16[128,8,1024]{2,1,0:T(8,128)(2,1)}, bf16[128,8,1024]{2,1,0:T(8,128)(2,1)S(1)}, u32[]{:S(2)}) copy-start(bf16[128,8,1024]{2,1,0:T(8,128)(2,1)S(1)} %all_to_all.26) | copy-start | bytes 6291460
  108.3 1.0 copy-start.5
  109.2 0.8 copy-start.8
  110.0 0.8 copy-start.9
  110.8 1.0 copy-start.17
  111.8 14.5 %copy-start.18 = (bf16[4096,128]{1,0:T(8,128)(2,1)S(1)}, bf16[4096,128]{1,0:T(8,128)(2,1)}, u32[]{:S(2)}) copy-start(bf16[4096,128]{1,0:T(8,128)(2,1)} %copy-done.17) | copy-start | bytes 3145732
  125.1 10.4 %copy-start.6 = (bf16[4096,128]{1,0:T(8,128)(2,1)S(1)}, bf16[4096,128]{1,0:T(8,128)(2,1)}, u32[]{:S(2)}) copy-start(bf16[4096,128]{1,0:T(8,128)(2,1)} %copy-done.5) | copy-start | bytes 3145732
  125.1 3.3 %collective-permute-start.9 = (bf16[3072,128]{1,0:T(8,128)(2,1)}, bf16[3072,128]{1,0:T(8,128)(2,1)S(1)}, u32[]{:S(2)}, u32[]{:S(2)}) collective-permute-start(bf16[3072,128]{1,0:T(8,128)(2,1)} %get-tuple-element.83), channel_id=1, source_target_pairs={{0,16},{16,0},{1,17},{17,1},{2,18},{18,2},{3,19},{19,3},{4,20},{20... | collective-permute-start | bytes 2359304 | tf_op jit(solution)/shard_map/ppermute | solution.py:370
  126.3 9.2 %collective-permute-start.8 = (bf16[4096,128]{1,0:T(8,128)(2,1)S(1)}, bf16[4096,128]{1,0:T(8,128)(2,1)}, u32[]{:S(2)}, u32[]{:S(2)}) collective-permute-start(bf16[4096,128]{1,0:T(8,128)(2,1)S(1)} %copy-done.18), channel_id=1, source_target_pairs={{0,16},{16,0},{1,17},{17,1},{2,18},{18,2},{3,19},{19,3},{4,20},{20... | collective-permute-start | bytes 3145736 | tf_op jit(solution)/shard_map/ppermute | solution.py:370
  130.6 19.6 %all-to-all-start.3 = ((bf16[64,48,128]{2,1,0:T(8,128)(2,1)}), bf16[64,48,128]{2,1,0:T(8,128)(2,1)S(1)}, u32[]{:S(2)}, u32[]{:S(2)}) async-start(bf16[64,48,128]{2,1,0:T(8,128)(2,1)} %bitcast.17), calls=%async_computation.3 | async-start | bytes 1572864 | tf_op jit(solution)/shard_map/all_to_all | solution.py:378
  150.3 21.1 %all-to-all-start.2 = ((bf16[64,64,128]{2,1,0:T(8,128)(2,1)}), bf16[64,64,128]{2,1,0:T(8,128)(2,1)S(1)}, u32[]{:S(2)}, u32[]{:S(2)}) async-start(bf16[64,64,128]{2,1,0:T(8,128)(2,1)} %bitcast.10), calls=%async_computation.2 | async-start | bytes 2097152 | tf_op jit(solution)/shard_map/all_to_all | solution.py:378
  171.8 32.9 %copy-start.30 = (bf16[32,512]{1,0:T(8,128)(2,1)S(1)}, bf16[32,512]{1,0:T(8,128)(2,1)}, u32[]{:S(2)}) copy-start(bf16[32,512]{1,0:T(8,128)(2,1)} %get-tuple-element.74) | copy-start | bytes 98308
  171.8 32.8 %copy-start.29 = (bf16[32,512]{1,0:T(8,128)(2,1)S(1)}, bf16[32,512]{1,0:T(8,128)(2,1)}, u32[]{:S(2)}) copy-start(bf16[32,512]{1,0:T(8,128)(2,1)} %get-tuple-element.75) | copy-start | bytes 98308
  171.8 35.1 %copy-start.28 = (bf16[32,512]{1,0:T(8,128)(2,1)S(1)}, bf16[32,512]{1,0:T(8,128)(2,1)}, u32[]{:S(2)}) copy-start(bf16[32,512]{1,0:T(8,128)(2,1)} %get-tuple-element.76) | copy-start | bytes 98308
  171.8 35.5 %copy-start.27 = (bf16[32,512]{1,0:T(8,128)(2,1)S(1)}, bf16[32,512]{1,0:T(8,128)(2,1)}, u32[]{:S(2)}) copy-start(bf16[32,512]{1,0:T(8,128)(2,1)} %get-tuple-element.77) | copy-start | bytes 98308
  201.0 18.4 %collective-permute-start.10 = (bf16[64,112,128]{2,1,0:T(8,128)(2,1)S(1)}, bf16[64,112,128]{2,1,0:T(8,128)(2,1)S(1)}, u32[]{:S(2)}, u32[]{:S(2)}) collective-permute-start(bf16[64,112,128]{2,1,0:T(8,128)(2,1)S(1)} %all_to_all.27.gathered), channel_id=1, source_target_pairs={{0,16},{16,0},{1,17},{17,1},{2,18},{18,2},{3,19},{19,3},{4,20},{20... | collective-permute-start | bytes 5505032 | tf_op jit(solution)/shard_map/ppermute | solution.py:370
  204.6 3.5 %collective-permute-start.4 = (bf16[32,512]{1,0:T(8,128)(2,1)S(1)}, bf16[32,512]{1,0:T(8,128)(2,1)S(1)}, u32[]{:S(2)}, u32[]{:S(2)}) collective-permute-start(bf16[32,512]{1,0:T(8,128)(2,1)S(1)} %copy-done.30), channel_id=1, source_target_pairs={{0,16},{32,48},{64,80},{96,112},{16,0},{48,32},{80,64},{112,96},{1... | collective-permute-start | bytes 98312 | tf_op jit(solution)/shard_map/ppermute | solution.py:352
  204.6 5.2 %collective-permute-start.5 = (bf16[32,512]{1,0:T(8,128)(2,1)S(1)}, bf16[32,512]{1,0:T(8,128)(2,1)S(1)}, u32[]{:S(2)}, u32[]{:S(2)}) collective-permute-start(bf16[32,512]{1,0:T(8,128)(2,1)S(1)} %copy-done.29), channel_id=1, source_target_pairs={{16,32},{48,64},{80,96},{32,16},{64,48},{96,80},{17,33},{49,65},{8... | collective-permute-start | bytes 98312 | tf_op jit(solution)/shard_map/ppermute | solution.py:352
  206.9 2.9 %collective-permute-start.6 = (bf16[32,512]{1,0:T(8,128)(2,1)S(1)}, bf16[32,512]{1,0:T(8,128)(2,1)S(1)}, u32[]{:S(2)}, u32[]{:S(2)}) collective-permute-start(bf16[32,512]{1,0:T(8,128)(2,1)S(1)} %copy-done.28), channel_id=1, source_target_pairs={{0,1},{2,3},{4,5},{6,7},{8,9},{10,11},{12,13},{14,15},{1,0},{3,2},... | collective-permute-start | bytes 98312 | tf_op jit(solution)/shard_map/ppermute | solution.py:352
  207.4 2.5 %collective-permute-start.7 = (bf16[32,512]{1,0:T(8,128)(2,1)S(1)}, bf16[32,512]{1,0:T(8,128)(2,1)S(1)}, u32[]{:S(2)}, u32[]{:S(2)}) collective-permute-start(bf16[32,512]{1,0:T(8,128)(2,1)S(1)} %copy-done.27), channel_id=1, source_target_pairs={{1,2},{3,4},{5,6},{7,8},{9,10},{11,12},{13,14},{2,1},{4,3},{6,5},{... | collective-permute-start | bytes 98312 | tf_op jit(solution)/shard_map/ppermute | solution.py:352
  208.1 1.8 copy-start.23
  209.9 0.6 copy-start.24
  209.9 0.6 copy-start.25
  209.9 0.6 copy-start.26
  210.5 6.5 %copy-start.14 = (s32[2]{0:T(128)S(1)}, s32[2]{0:T(128)}, u32[]{:S(2)}) copy-start(s32[2]{0:T(128)} %pad_add_fusion.where) | copy-start | bytes 28

commit v2 on v1

--- a/solution.py
+++ b/solution.py
@@ -14,6 +14,7 @@
 F32 = jnp.float32
 LANES = 128
 CHUNK = 1024
+BACK_CHUNK = 2048
 SMALL = 32
 LARGE = 60
 CAPACITY = 8
@@ -107,15 +108,16 @@
     target_side[...] = dot(nodes[...], target_weight[...]).astype(BF)
 
 
-def chunk(turn):
-    return slice(turn * CHUNK, (turn + 1) * CHUNK)
+def chunk(turn, length):
+    return slice(turn * length, (turn + 1) * length)
 
 
 def forward_kernel(
     where, halo_0, halo_1, halo_2, halo_3, own_source, target_side, nodes, cotangent, edge_source, edge_target, slot,
     source_weight, edge_weight, inner_far, outer_far,
     edge_hidden, edge_slope, message_slope, aggregate, node_hidden, node_slope, refined, sent,
-    sides, active, spread, inner_weight, outer_weight, hidden_kept, slope_kept, message_kept, weight_sems, sems,
+    sides, active, spread, inner_weight, outer_weight, hidden_kept, slope_kept, message_kept,
+    aggregate_kept, node_kept, weight_sems, sems, node_sems,
 ):
     fetches = [
         pltpu.make_async_copy(inner_far, inner_weight, weight_sems.at[0]),
@@ -136,7 +138,7 @@
     group = CHUNK // LANES
     stores = []
     for turn in range(edges // CHUNK):
-        span = chunk(turn)
+        span = chunk(turn, CHUNK)
         picks = []
         for at in range(turn * group, (turn + 1) * group):
             senders = edge_source[at : at + 1, :]
@@ -157,14 +159,19 @@
             stores.append(pltpu.make_async_copy(kept.at[span, :], out.at[span, :], sems.at[number, turn]))
             stores[-1].start()
     gathered = dot(spread[...], active[...]).astype(BF)
-    aggregate[...] = gathered
+    aggregate_kept[...] = gathered
+    stores.append(pltpu.make_async_copy(aggregate_kept, aggregate, node_sems.at[0]))
+    stores[-1].start()
     for fetch in fetches:
         fetch.wait()
     linear = dot(nodes[...], inner_weight[:width, :]) + dot(gathered, inner_weight[width:, :])
     hidden, slope = gates(linear)
     hidden = hidden.astype(BF)
-    node_hidden[...] = hidden
-    node_slope[...] = slope.astype(BF)
+    node_kept[0] = hidden
+    node_kept[1] = slope.astype(BF)
+    for number, out in enumerate((node_hidden, node_slope)):
+        stores.append(pltpu.make_async_copy(node_kept.at[number], out, node_sems.at[1 + number]))
+        stores[-1].start()
     result = (nodes[...].astype(F32) + dot(hidden, outer_weight[...])).astype(BF)
     refined[...] = result
     place = hot(iota((sent.shape[0], rows), 0) == slot[...])
@@ -237,11 +244,11 @@
     rows, _ = nodes.shape
     table = grad_sources.shape[0]
     edges = slope_kept.shape[0]
-    turns = edges // CHUNK
-    group = CHUNK // LANES
+    turns = edges // BACK_CHUNK
+    group = BACK_CHUNK // LANES
     fetches = []
     for turn in range(turns):
-        span = chunk(turn)
+        span = chunk(turn, BACK_CHUNK)
         for number, (far, kept) in enumerate(((message_slope, message_kept), (edge_slope, slope_kept))):
             fetches.append(pltpu.make_async_copy(far.at[span, :], kept.at[span, :], sems.at[number, turn]))
     fetches.append(pltpu.make_async_copy(edge_hidden, hidden_kept, sems.at[2, 0]))
@@ -253,7 +260,7 @@
     for at, halo in zip(received, (halo_0, halo_1, halo_2, halo_3)):
         extended[block(at, rows, length), :] = halo[...]
     for turn in range(turns):
-        span = chunk(turn)
+        span = chunk(turn, BACK_CHUNK)
         picks = []
         for at in range(turn * group, (turn + 1) * group):
             senders = edge_source[at : at + 1, :]
@@ -427,10 +434,11 @@
         [(edge_block, BF)] * 3 + [(node_block, BF)] * 4 + [((slots, 2 * width), BF)],
         *halo, own_source, target_side, nodes, cotangent, senders, receivers, slot,
         source_weight, edge_weight, inner_weight, outer_weight,
-        far_in=2, far_out=3,
+        far_in=2, far_out=6,
         scratch=[((extended + rows, width), BF), (edge_block, BF), ((rows, edges), BF)]
-        + [((2 * width, width), BF), ((width, width), BF)] + [(edge_block, BF)] * 3,
-        sems=[(2,), (3, edges // CHUNK)],
+        + [((2 * width, width), BF), ((width, width), BF)] + [(edge_block, BF)] * 3
+        + [(node_block, BF), ((2, rows, width), BF)],
+        sems=[(2,), (3, edges // CHUNK), (3,)],
         where=where,
     )
     arrived = trade_slots(sent, devices)
@@ -458,7 +466,7 @@
         edge_slope, message_slope, edge_hidden,
         far_in=3,
         scratch=[(edge_block, BF)] * 5 + [((extended, edges), BF), ((rows, edges), BF), ((extended, width), BF)],
-        sems=[(3, edges // CHUNK)],
+        sems=[(3, edges // BACK_CHUNK)],
         where=where, scale=scale,
     )
     halo_back = trade_halo(back)

time: 226 us -> 226 us (level)
  no operation moved by 1% of the time
where the time goes in v2:
time: 226 us; the launch traced here: 222 us
  blocking collectives  106 us (47%)
  Pallas kernels  46.5 us (21%)
  waiting for transfers between devices  32.9 us (15%)
  starting transfers between devices  24.5 us (11%)
  other arithmetic  5.65 us (2%)
  local copies, waits for them, and re-layouts  5.07 us (2%)
    all_to_all x2, blocking collectives, trade_slots(): moved = lax.all_to_all(shaped, ALL, split_axis=0, concat_axis=0, tiled=True)  76.7 us
    pallas_call x9, Pallas kernels, call(): pl.pallas_call(body, in_specs=specs, out_specs=[far] * far_out + [near] *...  46.5 us
    all_to_all x1, blocking collectives, trade_chips(): return lax.all_to_all(value, CHIPS, split_axis=0, concat_axis=0, tiled=True)  29.4 us
    all_to_all x2, waiting for transfers between devices, trade_chips(): return lax.all_to_all(value, CHIPS, split_axis=0, concat_axis=0, tiled=True)  29 us
    ppermute x8, starting transfers between devices, swapped(): return lax.ppermute(value, axis, pairs)  10.3 us
    all_to_all x2, starting transfers between devices, trade_chips(): return lax.all_to_all(value, CHIPS, split_axis=0, concat_axis=0, tiled=True)  9.52 us
    unnamed x62, local copies, waits for them, and re-layouts  4.83 us
    convert_element_type x2, other arithmetic, paired(): return (keep.astype(F32) + across(give).astype(F32)).astype(BF)  4.68 us
  transfers between devices with their start and end apart: 13, of which 5 were waited for; matrix products, arithmetic and copies ran while one was open for 2% of the time, Pallas kernels for 5%

profile of v2, /device:TPU:1, one launch (start us, length us, event | category | flops | bytes accessed | tf_op | source)
XLA Modules:
  0.0 222.0 jit_solution(5325872453956700610)
XLA Ops:
  0.6 0.6 pad_add_fusion.where
  1.3 2.0 shard_map.188
  3.2 1.4 collective-permute-start
  4.6 3.5 %collective-permute-start.1 = (bf16[32,512]{1,0:T(8,128)(2,1)}, bf16[32,512]{1,0:T(8,128)(2,1)S(1)}, u32[]{:S(2)}, u32[]{:S(2)}) collective-permute-start(bf16[32,512]{1,0:T(8,128)(2,1)} %get-tuple-element.53), channel_id=1, source_target_pairs={{16,32},{48,64},{80,96},{32,16},{64,48},{96,80},{17,33},{49,65},{8... | collective-permute-start | bytes 98312 | tf_op jit(solution)/shard_map/ppermute | solution.py:359
  8.2 1.4 collective-permute-start.2
  9.5 0.7 collective-permute-start.3
  10.2 2.9 %shard_map.189 = (s32[1,512]{1,0:T(1,128)}, bf16[512,512]{1,0:T(8,128)(2,1)}, bf16[512,512]{1,0:T(8,128)(2,1)}) custom-call(s32[4,128]{1,0:T(4,128)} %bitcast.23, bf16[512,512]{1,0:T(8,128)(2,1)} %nodes.9, bf16[512,512]{1,0:T(8,128)(2,1)} %source_weight.7, bf16[512,512]{1,0:T(8,128)(2,1)} %target_weight.3), custom_call_target="tpu_custom_call" | custom-call | tf_op jit(solution)/shard_map/pallas_call | solution.py:343
  13.2 0.6 copy-done.19
  13.8 0.0 copy-done.21
  13.8 0.0 copy-done.22
  13.8 12.5 %shard_map.190 = (bf16[2048,512]{1,0:T(8,128)(2,1)}, bf16[2048,512]{1,0:T(8,128)(2,1)}, bf16[2048,512]{1,0:T(8,128)(2,1)}, bf16[512,512]{1,0:T(8,128)(2,1)}, bf1...) custom-call(s32[2]{0:T(128)} %pad_add_fusion.where, ...), custom_call_target="tpu_custom_call" | custom-call | tf_op jit(solution)/shard_map/pallas_call | solution.py:343
  26.3 0.0 copy-start.7
  26.3 42.5 %all_to_all.25 = bf16[128,8,1024]{2,1,0:T(8,128)(2,1)S(1)} all-to-all(bf16[128,8,1024]{2,1,0:T(8,128)(2,1)} %bitcast.18), channel_id=1, replica_groups=mesh['z'=4,'core'=2,'x'=4,'y'=4] {'z','core','x','y'}, dimensions={0} | all-to-all | bytes 4194304 | tf_op jit(solution)/shard_map/all_to_all | solution.py:372
  68.8 1.5 shard_map.191
  70.3 0.0 copy-start.1
  70.4 0.0 copy-start.4
  70.5 34.2 %all_to_all.26 = bf16[128,8,1024]{2,1,0:T(8,128)(2,1)S(1)} all-to-all(bf16[128,8,1024]{2,1,0:T(8,128)(2,1)S(1)} %bitcast.15), channel_id=1, replica_groups=mesh['z'=4,'core'=2,'x'=4,'y'=4] {'z','core','x','y'}, dimensions={0} | all-to-all | bytes 4194304 | tf_op jit(solution)/shard_map/all_to_all | solution.py:372
  104.7 3.0 %shard_map.192 = (bf16[512,512]{1,0:T(8,128)(2,1)S(1)}, bf16[512,512]{1,0:T(8,128)(2,1)S(1)}, bf16[4096,128]{1,0:T(8,128)(2,1)S(1)}, bf16[4096,128]{1,0:T(8,128)(2,1)S(1)}) custom-call(s32[2]{0:T(128)S(1)} %copy-done.13, bf16[1024,1024]{1,0:T(8,128)(2,1)S(1)} %bitcast.12, s32[1,512]{1,0:T(1,128)S(1)} %copy-done.15, bf16[512,512]{1,0:T(8,128)(2,1)S(1)} %copy-done.3, ...), custom_call_target="tpu_custom_call" | custom-call | tf_op jit(solution)/shard_map/pallas_call | solution.py:343
  107.8 1.0 copy-done.5
  108.8 0.8 copy-done.8
  109.6 0.8 copy-done.9
  110.3 1.0 copy-done.17
  111.3 13.1 %shard_map.193 = (bf16[3072,128]{1,0:T(8,128)(2,1)}, bf16[3072,128]{1,0:T(8,128)(2,1)}, bf16[640,512]{1,0:T(8,128)(2,1)}, bf16[512,512]{1,0:T(8,128)(2,1)}, bf16...) custom-call(s32[2]{0:T(128)} %pad_add_fusion.where, ...), custom_call_target="tpu_custom_call" | custom-call | tf_op jit(solution)/shard_map/pallas_call | solution.py:343
  124.4 1.2 collective-permute-start.9
  125.6 0.1 collective-permute-start.8
  125.7 2.0 collective-permute-done.9
  127.7 2.2 add_convert_fusion.1
  129.9 4.9 %all-to-all-start.3 = ((bf16[64,48,128]{2,1,0:T(8,128)(2,1)}), bf16[64,48,128]{2,1,0:T(8,128)(2,1)S(1)}, u32[]{:S(2)}, u32[]{:S(2)}) async-start(bf16[64,48,128]{2,1,0:T(8,128)(2,1)} %bitcast.17), calls=%async_computation.3 | async-start | bytes 1572864 | tf_op jit(solution)/shard_map/all_to_all | solution.py:385
  134.8 2.5 %add_convert_fusion = bf16[4096,128]{1,0:T(8,128)(2,1)} fusion(bf16[4096,128]{1,0:T(8,128)(2,1)} %collective-permute-done.8, bf16[4096,128]{1,0:T(8,128)(2,1)S(1)} %copy-done.6), kind=kLoop, calls=%fused_computation | loop fusion | flops 2097152 | bytes 3145728 | tf_op jit(solution)/shard_map/convert_element_type | solution.py:381
  137.3 12.8 %all-to-all-done.3 = bf16[64,48,128]{2,1,0:T(8,128)(2,1)S(1)} async-done(((bf16[64,48,128]{2,1,0:T(8,128)(2,1)}), bf16[64,48,128]{2,1,0:T(8,128)(2,1)S(1)}, u32[]{:S(2)}, u32[]{:S(2)}) %all-to-all-start.3) | async-done | bytes 786464 | tf_op jit(solution)/shard_map/all_to_all | solution.py:385
  150.1 4.7 %all-to-all-start.2 = ((bf16[64,64,128]{2,1,0:T(8,128)(2,1)}), bf16[64,64,128]{2,1,0:T(8,128)(2,1)S(1)}, u32[]{:S(2)}, u32[]{:S(2)}) async-start(bf16[64,64,128]{2,1,0:T(8,128)(2,1)} %bitcast.10), calls=%async_computation.2 | async-start | bytes 2097152 | tf_op jit(solution)/shard_map/all_to_all | solution.py:385
  154.7 0.1 reduce_sum.25
  154.9 16.3 %all-to-all-done.2 = bf16[64,64,128]{2,1,0:T(8,128)(2,1)S(1)} async-done(((bf16[64,64,128]{2,1,0:T(8,128)(2,1)}), bf16[64,64,128]{2,1,0:T(8,128)(2,1)S(1)}, u32[]{:S(2)}, u32[]{:S(2)}) %all-to-all-start.2) | async-done | bytes 1048608 | tf_op jit(solution)/shard_map/all_to_all | solution.py:385
  171.2 0.2 reduce_sum.24
  171.3 0.2 broadcast_in_dim.2
  171.6 29.4 %all_to_all.27.gathered = bf16[64,112,128]{2,1,0:T(8,128)(2,1)S(1)} all-to-all(bf16[64,112,128]{2,1,0:T(8,128)(2,1)S(1)} %broadcast_in_dim.2), channel_id=1, replica_groups=mesh['z'=4,'core'=2,'x'=4,'y'=4] {'z','x','y'}, dimensions={0} | all-to-all | bytes 3670016 | tf_op jit(solution)/shard_map/all_to_all | solution.py:385
  201.1 3.4 %collective-permute-start.10 = (bf16[64,112,128]{2,1,0:T(8,128)(2,1)S(1)}, bf16[64,112,128]{2,1,0:T(8,128)(2,1)S(1)}, u32[]{:S(2)}, u32[]{:S(2)}) collective-permute-start(bf16[64,112,128]{2,1,0:T(8,128)(2,1)S(1)} %all_to_all.27.gathered), channel_id=1, source_target_pairs={{0,16},{16,0},{1,17},{17,1},{2,18},{18,2},{3,19},{19,3},{4,20},{20... | collective-permute-start | bytes 5505032 | tf_op jit(solution)/shard_map/ppermute | solution.py:377
  204.4 2.3 %collective-permute-start.5 = (bf16[32,512]{1,0:T(8,128)(2,1)S(1)}, bf16[32,512]{1,0:T(8,128)(2,1)S(1)}, u32[]{:S(2)}, u32[]{:S(2)}) collective-permute-start(bf16[32,512]{1,0:T(8,128)(2,1)S(1)} %copy-done.29), channel_id=1, source_target_pairs={{16,32},{48,64},{80,96},{32,16},{64,48},{96,80},{17,33},{49,65},{8... | collective-permute-start | bytes 98312 | tf_op jit(solution)/shard_map/ppermute | solution.py:359
  206.7 0.4 collective-permute-start.6
  207.2 0.7 collective-permute-start.7
  207.8 0.1 collective-permute-done.4.back_0
  207.9 1.8 collective-permute-done.5.back_1
  209.7 0.6 copy-done.24
  210.3 0.0 copy-done.25
  210.3 0.0 copy-done.26
  210.3 6.5 %shard_map.194 = (bf16[512,512]{1,0:T(8,128)(2,1)}, f32[512,512]{1,0:T(8,128)}) custom-call(s32[2]{0:T(128)} %pad_add_fusion.where, bf16[1024,1024]{1,0:T(8,128)(2,1)} %bitcast.13, s32[1,512]{1,0:T(1,128)} %get-tuple-element.58.slot, bf16[512,512]{1,0:T(8,128)(2,1)} %cotangent.5, bf16[512,512]{1,0:T(8,128)(2,1)} %get-tuple-element.61.refined, ...), custom_call_target="tpu_custom_call" | custom-call | tf_op jit(solution)/shard_map/pallas_call | solution.py:343
  216.8 2.5 %shard_map.195 = (f32[512,512]{1,0:T(8,128)}, f32[512,512]{1,0:T(8,128)}, f32[512,512]{1,0:T(8,128)}, f32[1024,512]{1,0:T(8,128)}, f32[512,512]{1,0:T(8,128)}, /*index=5*/f32[512,512]{1,0:T(8,128)}) custom-call(s32[2]{0:T(128)S(1)} %copy-done.14, bf16[64,112,128]{2,1,0:T(8,128)(2,1)S(1)} %all_to_all.27.gathered), custom_call_target="tpu_custom_call" | custom-call | tf_op jit(solution)/shard_map/pallas_call | solution.py:343
  219.3 2.5 %shard_map.196 = (f32[512,512]{1,0:T(8,128)}, f32[512,512]{1,0:T(8,128)}, f32[512,512]{1,0:T(8,128)}, f32[1024,512]{1,0:T(8,128)}, f32[512,512]{1,0:T(8,128)}, /*index=5*/f32[512,512]{1,0:T(8,128)}) custom-call(s32[2]{0:T(128)S(1)} %copy-done.14, ...), custom_call_target="tpu_custom_call", output_to_operand_aliasing={{0}: (2, {}), {1}: (3, {}), {2}: (4, {}), {3}: (5, {}), {4}... | custom-call | tf_op jit(solution)/shard_map/pallas_call | solution.py:343
  (59 shorter events, 0.1 us)
Async XLA Ops:
  3.2 9.9 %collective-permute-start = (bf16[32,512]{1,0:T(8,128)(2,1)}, bf16[32,512]{1,0:T(8,128)(2,1)S(1)}, u32[]{:S(2)}, u32[]{:S(2)}) collective-permute-start(bf16[32,512]{1,0:T(8,128)(2,1)} %get-tuple-element.52), channel_id=1, source_target_pairs={{0,16},{32,48},{64,80},{96,112},{16,0},{48,32},{80,64},{112,96},{1... | collective-permute-start | bytes 98312 | tf_op jit(solution)/shard_map/ppermute | solution.py:359
  4.6 8.5 %collective-permute-start.1 = (bf16[32,512]{1,0:T(8,128)(2,1)}, bf16[32,512]{1,0:T(8,128)(2,1)S(1)}, u32[]{:S(2)}, u32[]{:S(2)}) collective-permute-start(bf16[32,512]{1,0:T(8,128)(2,1)} %get-tuple-element.53), channel_id=1, source_target_pairs={{16,32},{48,64},{80,96},{32,16},{64,48},{96,80},{17,33},{49,65},{8... | collective-permute-start | bytes 98312 | tf_op jit(solution)/shard_map/ppermute | solution.py:359
  8.2 5.0 %collective-permute-start.2 = (bf16[32,512]{1,0:T(8,128)(2,1)}, bf16[32,512]{1,0:T(8,128)(2,1)S(1)}, u32[]{:S(2)}, u32[]{:S(2)}) collective-permute-start(bf16[32,512]{1,0:T(8,128)(2,1)} %get-tuple-element.54), channel_id=1, source_target_pairs={{0,1},{2,3},{4,5},{6,7},{8,9},{10,11},{12,13},{14,15},{1,0},{3,2},... | collective-permute-start | bytes 98312 | tf_op jit(solution)/shard_map/ppermute | solution.py:359
  9.5 3.6 %collective-permute-start.3 = (bf16[32,512]{1,0:T(8,128)(2,1)}, bf16[32,512]{1,0:T(8,128)(2,1)S(1)}, u32[]{:S(2)}, u32[]{:S(2)}) collective-permute-start(bf16[32,512]{1,0:T(8,128)(2,1)} %get-tuple-element.55), channel_id=1, source_target_pairs={{1,2},{3,4},{5,6},{7,8},{9,10},{11,12},{13,14},{2,1},{4,3},{6,5},{... | collective-permute-start | bytes 98312 | tf_op jit(solution)/shard_map/ppermute | solution.py:359
  13.1 0.6 copy-start.19
  13.2 0.6 copy-start.20
  13.2 0.6 copy-start.21
  13.2 0.6 copy-start.22
  26.3 42.5 %copy-start.7 = (bf16[512,512]{1,0:T(8,128)(2,1)S(1)}, bf16[512,512]{1,0:T(8,128)(2,1)}, u32[]{:S(2)}) copy-start(bf16[512,512]{1,0:T(8,128)(2,1)} %weight.1) | copy-start | bytes 1572868
  26.3 42.5 %copy-start.16 = (s32[1,1024]{1,0:T(1,128)S(1)}, s32[1,1024]{1,0:T(1,128)}, u32[]{:S(2)}) copy-start(s32[1,1024]{1,0:T(1,128)} %param.19) | copy-start | bytes 12292
  70.3 34.3 %copy-start.1 = (bf16[512,512]{1,0:T(8,128)(2,1)S(1)}, bf16[512,512]{1,0:T(8,128)(2,1)}, u32[]{:S(2)}) copy-start(bf16[512,512]{1,0:T(8,128)(2,1)} %nodes.9) | copy-start | bytes 1572868
  70.4 34.3 %copy-start.2 = (bf16[1024,512]{1,0:T(8,128)(2,1)S(1)}, bf16[1024,512]{1,0:T(8,128)(2,1)}, u32[]{:S(2)}) copy-start(bf16[1024,512]{1,0:T(8,128)(2,1)} %inner_weight.3) | copy-start | bytes 3145732
  70.4 34.3 %copy-start.3 = (bf16[512,512]{1,0:T(8,128)(2,1)S(1)}, bf16[512,512]{1,0:T(8,128)(2,1)}, u32[]{:S(2)}) copy-start(bf16[512,512]{1,0:T(8,128)(2,1)} %cotangent.5) | copy-start | bytes 1572868
  70.4 34.3 %copy-start.4 = (bf16[512,512]{1,0:T(8,128)(2,1)S(1)}, bf16[512,512]{1,0:T(8,128)(2,1)}, u32[]{:S(2)}) copy-start(bf16[512,512]{1,0:T(8,128)(2,1)} %outer_weight.1) | copy-start | bytes 1572868
  70.4 34.3 %copy-start.10 = (bf16[512,512]{1,0:T(8,128)(2,1)S(1)}, bf16[512,512]{1,0:T(8,128)(2,1)}, u32[]{:S(2)}) copy-start(bf16[512,512]{1,0:T(8,128)(2,1)} %get-tuple-element.62.aggregate) | copy-start | bytes 1572868
  70.4 34.3 %copy-start.11 = (bf16[512,512]{1,0:T(8,128)(2,1)S(1)}, bf16[512,512]{1,0:T(8,128)(2,1)}, u32[]{:S(2)}) copy-start(bf16[512,512]{1,0:T(8,128)(2,1)} %get-tuple-element.63.node_hidden) | copy-start | bytes 1572868
  70.4 34.3 %copy-start.12 = (bf16[512,512]{1,0:T(8,128)(2,1)S(1)}, bf16[512,512]{1,0:T(8,128)(2,1)}, u32[]{:S(2)}) copy-start(bf16[512,512]{1,0:T(8,128)(2,1)} %get-tuple-element.64.node_slope) | copy-start | bytes 1572868
  70.4 34.3 %copy-start.13 = (s32[2]{0:T(128)S(1)}, s32[2]{0:T(128)}, u32[]{:S(2)}) copy-start(s32[2]{0:T(128)} %pad_add_fusion.where) | copy-start | bytes 28
  70.4 34.3 %copy-start.15 = (s32[1,512]{1,0:T(1,128)S(1)}, s32[1,512]{1,0:T(1,128)}, u32[]{:S(2)}) copy-start(s32[1,512]{1,0:T(1,128)} %get-tuple-element.58.slot) | copy-start | bytes 6148
  104.7 3.1 %copy-start = (bf16[128,8,1024]{2,1,0:T(8,128)(2,1)}, bf16[128,8,1024]{2,1,0:T(8,128)(2,1)S(1)}, u32[]{:S(2)}) copy-start(bf16[128,8,1024]{2,1,0:T(8,128)(2,1)S(1)} %all_to_all.26) | copy-start | bytes 6291460
  107.8 1.0 copy-start.5
  108.8 0.8 copy-start.8
  109.5 0.8 copy-start.9
  110.3 1.0 copy-start.17
  111.3 14.3 %copy-start.18 = (bf16[4096,128]{1,0:T(8,128)(2,1)S(1)}, bf16[4096,128]{1,0:T(8,128)(2,1)}, u32[]{:S(2)}) copy-start(bf16[4096,128]{1,0:T(8,128)(2,1)} %copy-done.17) | copy-start | bytes 3145732
  124.4 10.4 %copy-start.6 = (bf16[4096,128]{1,0:T(8,128)(2,1)S(1)}, bf16[4096,128]{1,0:T(8,128)(2,1)}, u32[]{:S(2)}) copy-start(bf16[4096,128]{1,0:T(8,128)(2,1)} %copy-done.5) | copy-start | bytes 3145732
  124.4 3.3 %collective-permute-start.9 = (bf16[3072,128]{1,0:T(8,128)(2,1)}, bf16[3072,128]{1,0:T(8,128)(2,1)S(1)}, u32[]{:S(2)}, u32[]{:S(2)}) collective-permute-start(bf16[3072,128]{1,0:T(8,128)(2,1)} %get-tuple-element.83), channel_id=1, source_target_pairs={{0,16},{16,0},{1,17},{17,1},{2,18},{18,2},{3,19},{19,3},{4,20},{20... | collective-permute-start | bytes 2359304 | tf_op jit(solution)/shard_map/ppermute | solution.py:377
  125.6 9.2 %collective-permute-start.8 = (bf16[4096,128]{1,0:T(8,128)(2,1)S(1)}, bf16[4096,128]{1,0:T(8,128)(2,1)}, u32[]{:S(2)}, u32[]{:S(2)}) collective-permute-start(bf16[4096,128]{1,0:T(8,128)(2,1)S(1)} %copy-done.18), channel_id=1, source_target_pairs={{0,16},{16,0},{1,17},{17,1},{2,18},{18,2},{3,19},{19,3},{4,20},{20... | collective-permute-start | bytes 3145736 | tf_op jit(solution)/shard_map/ppermute | solution.py:377
  129.9 20.1 %all-to-all-start.3 = ((bf16[64,48,128]{2,1,0:T(8,128)(2,1)}), bf16[64,48,128]{2,1,0:T(8,128)(2,1)S(1)}, u32[]{:S(2)}, u32[]{:S(2)}) async-start(bf16[64,48,128]{2,1,0:T(8,128)(2,1)} %bitcast.17), calls=%async_computation.3 | async-start | bytes 1572864 | tf_op jit(solution)/shard_map/all_to_all | solution.py:385
  150.1 21.1 %all-to-all-start.2 = ((bf16[64,64,128]{2,1,0:T(8,128)(2,1)}), bf16[64,64,128]{2,1,0:T(8,128)(2,1)S(1)}, u32[]{:S(2)}, u32[]{:S(2)}) async-start(bf16[64,64,128]{2,1,0:T(8,128)(2,1)} %bitcast.10), calls=%async_computation.2 | async-start | bytes 2097152 | tf_op jit(solution)/shard_map/all_to_all | solution.py:385
  171.6 32.8 %copy-start.30 = (bf16[32,512]{1,0:T(8,128)(2,1)S(1)}, bf16[32,512]{1,0:T(8,128)(2,1)}, u32[]{:S(2)}) copy-start(bf16[32,512]{1,0:T(8,128)(2,1)} %get-tuple-element.74) | copy-start | bytes 98308
  171.6 32.8 %copy-start.29 = (bf16[32,512]{1,0:T(8,128)(2,1)S(1)}, bf16[32,512]{1,0:T(8,128)(2,1)}, u32[]{:S(2)}) copy-start(bf16[32,512]{1,0:T(8,128)(2,1)} %get-tuple-element.75) | copy-start | bytes 98308
  171.6 35.1 %copy-start.28 = (bf16[32,512]{1,0:T(8,128)(2,1)S(1)}, bf16[32,512]{1,0:T(8,128)(2,1)}, u32[]{:S(2)}) copy-start(bf16[32,512]{1,0:T(8,128)(2,1)} %get-tuple-element.76) | copy-start | bytes 98308
  171.6 35.5 %copy-start.27 = (bf16[32,512]{1,0:T(8,128)(2,1)S(1)}, bf16[32,512]{1,0:T(8,128)(2,1)}, u32[]{:S(2)}) copy-start(bf16[32,512]{1,0:T(8,128)(2,1)} %get-tuple-element.77) | copy-start | bytes 98308
  201.1 18.2 %collective-permute-start.10 = (bf16[64,112,128]{2,1,0:T(8,128)(2,1)S(1)}, bf16[64,112,128]{2,1,0:T(8,128)(2,1)S(1)}, u32[]{:S(2)}, u32[]{:S(2)}) collective-permute-start(bf16[64,112,128]{2,1,0:T(8,128)(2,1)S(1)} %all_to_all.27.gathered), channel_id=1, source_target_pairs={{0,16},{16,0},{1,17},{17,1},{2,18},{18,2},{3,19},{19,3},{4,20},{20... | collective-permute-start | bytes 5505032 | tf_op jit(solution)/shard_map/ppermute | solution.py:377
  204.4 3.5 %collective-permute-start.4 = (bf16[32,512]{1,0:T(8,128)(2,1)S(1)}, bf16[32,512]{1,0:T(8,128)(2,1)S(1)}, u32[]{:S(2)}, u32[]{:S(2)}) collective-permute-start(bf16[32,512]{1,0:T(8,128)(2,1)S(1)} %copy-done.30), channel_id=1, source_target_pairs={{0,16},{32,48},{64,80},{96,112},{16,0},{48,32},{80,64},{112,96},{1... | collective-permute-start | bytes 98312 | tf_op jit(solution)/shard_map/ppermute | solution.py:359
  204.4 5.2 %collective-permute-start.5 = (bf16[32,512]{1,0:T(8,128)(2,1)S(1)}, bf16[32,512]{1,0:T(8,128)(2,1)S(1)}, u32[]{:S(2)}, u32[]{:S(2)}) collective-permute-start(bf16[32,512]{1,0:T(8,128)(2,1)S(1)} %copy-done.29), channel_id=1, source_target_pairs={{16,32},{48,64},{80,96},{32,16},{64,48},{96,80},{17,33},{49,65},{8... | collective-permute-start | bytes 98312 | tf_op jit(solution)/shard_map/ppermute | solution.py:359
  206.7 2.9 %collective-permute-start.6 = (bf16[32,512]{1,0:T(8,128)(2,1)S(1)}, bf16[32,512]{1,0:T(8,128)(2,1)S(1)}, u32[]{:S(2)}, u32[]{:S(2)}) collective-permute-start(bf16[32,512]{1,0:T(8,128)(2,1)S(1)} %copy-done.28), channel_id=1, source_target_pairs={{0,1},{2,3},{4,5},{6,7},{8,9},{10,11},{12,13},{14,15},{1,0},{3,2},... | collective-permute-start | bytes 98312 | tf_op jit(solution)/shard_map/ppermute | solution.py:359
  207.2 2.5 %collective-permute-start.7 = (bf16[32,512]{1,0:T(8,128)(2,1)S(1)}, bf16[32,512]{1,0:T(8,128)(2,1)S(1)}, u32[]{:S(2)}, u32[]{:S(2)}) collective-permute-start(bf16[32,512]{1,0:T(8,128)(2,1)S(1)} %copy-done.27), channel_id=1, source_target_pairs={{1,2},{3,4},{5,6},{7,8},{9,10},{11,12},{13,14},{2,1},{4,3},{6,5},{... | collective-permute-start | bytes 98312 | tf_op jit(solution)/shard_map/ppermute | solution.py:359
  207.9 1.8 copy-start.23
  209.7 0.6 copy-start.24
  209.7 0.6 copy-start.25
  209.7 0.6 copy-start.26
  210.3 6.5 %copy-start.14 = (s32[2]{0:T(128)S(1)}, s32[2]{0:T(128)}, u32[]{:S(2)}) copy-start(s32[2]{0:T(128)} %pad_add_fusion.where) | copy-start | bytes 28
